TPU v7x, 256 devices: a whole 4x4x8 slice. The times are simulated.
256 devices in a mesh: ctx: 32 (over x, y, core), head: 8 (over z).
Axes of the slice: x: 4, y: 4, z: 8, core: 2. Of those that a mesh axis runs over, the one named last changes fastest.
Arguments:
- queries: bfloat16 [65536, 2048], P(('ctx', 'head')), may hold values from -6 to 6
- key_vectors: bfloat16 [65536, 2048], P(('ctx', 'head')), may hold values from -6 to 6
- value_vectors: bfloat16 [65536, 2048], P(('ctx', 'head')), may hold values from -6 to 6
- level_codes: int32 [65536, 6], P('ctx'), may hold values from 0 to 15
- level_table: bfloat16 [16, 16], replicated, may hold values from 0.25 to 2
- out_gain: float32 [16, 128], replicated, may hold values from 0.5 to 1.5
Outputs:
- attended: bfloat16 [65536, 2048], P(('ctx', 'head'))
All inputs are finite; a program needn't handle non-finite values.
Results may differ from a plain program's by a relative error of at most 0.005.
Values may be sent and summed in bfloat16 or wider, within the bound.
No kernel may reach another device: no remote copies, remote signals or barrier semaphores. Data moves between devices by JAX's collectives and lax.ppermute only.
A program may use at most 64 MiB of HBM per device.

v0:
```python
import functools

import jax
import jax.numpy as jnp
from jax import lax
from jax.experimental import pallas as pl
from jax.experimental.pallas import tpu as pltpu
from jax.sharding import Mesh, PartitionSpec as P


HEADS = 16
DH = 128
LEVELS = 6
CODES = 16
NEAR = 3
FAR = 2
SIDE = 8
PER = HEADS // SIDE
EPSILON = 1e-06
BF = jnp.bfloat16
F32 = jnp.float32


VMEM_SPEC = pl.BlockSpec(memory_space=pltpu.VMEM)
SMEM_SPEC = pl.BlockSpec(memory_space=pltpu.SMEM)
HBM_SPEC = pl.BlockSpec(memory_space=pltpu.HBM)
DMA = pltpu.SemaphoreType.DMA


def sds(shape, dtype):
    return jax.ShapeDtypeStruct(shape, dtype)


def call(kernel, outs, in_specs, cost, out_specs=None, scratch=(), alias=None):
    return pl.pallas_call(
        kernel,
        out_shape=outs,
        in_specs=in_specs,
        out_specs=jax.tree.map(lambda _: VMEM_SPEC, outs) if out_specs is None else out_specs,
        scratch_shapes=scratch,
        input_output_aliases=alias or {},
        compiler_params=pltpu.CompilerParams(vmem_limit_bytes=20 << 20),
        cost_estimate=pl.CostEstimate(flops=cost[0], bytes_accessed=cost[1], transcendentals=0),
    )


def in_hbm(value):
    return pltpu.with_memory_space_constraint(value, pltpu.HBM)


def head_cols(h):
    return pl.ds(h * DH, DH)


def dynamic_cols(h):
    return pl.ds(pl.multiple_of(h * DH, DH), DH)


LOADS = 4


def state_kernel(k_hbm, v_hbm, s_ref, k_ref, v_ref, sems):
    width = HEADS * DH // LOADS
    copies = []
    for i in range(LOADS):
        cols = pl.ds(i * width, width)
        pair = [
            pltpu.make_async_copy(k_hbm.at[:, cols], k_ref.at[:, cols], sems.at[0, i]),
            pltpu.make_async_copy(v_hbm.at[:, cols], v_ref.at[:, cols], sems.at[1, i]),
        ]
        for copy in pair:
            copy.start()
        copies.append(pair)
    for i in range(LOADS):
        for copy in copies[i]:
            copy.wait()
        for h in range(i * HEADS // LOADS, (i + 1) * HEADS // LOADS):
            s = lax.dot_general(
                k_ref[:, head_cols(h)], v_ref[:, head_cols(h)], (((0,), (0,)), ((), ())),
                preferred_element_type=F32,
            )
            s_ref[h] = s.astype(BF)


def local_kernel(
    q_hbm, k_hbm, v_hbm, codes_ref, table_ref, acc_hbm, qw_hbm, q_ref, k_ref, v_ref, acc_ref, qw_ref, sems, acc_sems, qw_sems
):
    width = HEADS * DH // LOADS
    per = HEADS // LOADS
    copies = []
    for i in range(LOADS):
        cols = pl.ds(i * width, width)
        group = [
            pltpu.make_async_copy(src.at[:, cols], dst.at[:, cols], sems.at[j, i])
            for j, (src, dst) in enumerate(((q_hbm, q_ref), (k_hbm, k_ref), (v_hbm, v_ref)))
        ]
        for copy in group:
            copy.start()
        copies.append(group)
    tokens = q_ref.shape[0]
    code_ids = lax.broadcasted_iota(jnp.int32, (CODES, tokens), 0)
    hits = [codes_ref[l : l + 1, :] == code_ids for l in range(LEVELS)]
    hits = [jnp.where(hit, 1.0, 0.0).astype(BF) for hit in hits]
    hits = jnp.concatenate(hits + [jnp.zeros((DH - LEVELS * CODES, tokens), BF)], axis=0)
    w = lax.dot_general(hits, table_ref[...], (((0,), (0,)), ((), ())), preferred_element_type=F32).astype(BF)
    rows = lax.broadcasted_iota(jnp.int32, (tokens, tokens), 0)
    cols = lax.broadcasted_iota(jnp.int32, (tokens, tokens), 1)
    keep = cols <= rows
    pick = lax.broadcasted_iota(jnp.int32, (DH, LEVELS * DH), 0)
    pick = pick - lax.broadcasted_iota(jnp.int32, (DH, LEVELS * DH), 1) // DH * HEADS
    stores = []
    for i in range(LOADS):
        for copy in copies[i]:
            copy.wait()
        for h in range(i * per, (i + 1) * per):
            spread = jnp.dot(w, jnp.where(pick == h, 1.0, 0.0).astype(BF), preferred_element_type=F32)
            q = q_ref[:, head_cols(h)]
            wide = q.astype(F32)
            for l in range(LEVELS):
                qw_ref[h, :, head_cols(l)] = (spread[:, l * DH : (l + 1) * DH] * wide).astype(BF)
            s = lax.dot_general(q, k_ref[:, head_cols(h)], (((1,), (1,)), ((), ())), preferred_element_type=F32)
            s = jnp.where(keep, s, 0.0).astype(BF)
            part = jnp.dot(s, v_ref[:, head_cols(h)], preferred_element_type=F32)
            acc_ref[:, head_cols(h)] = spread[:, :DH] * part
        cols = pl.ds(i * width, width)
        heads = pl.ds(i * per, per)
        for store in (
            pltpu.make_async_copy(acc_ref.at[:, cols], acc_hbm.at[:, cols], acc_sems.at[i]),
            pltpu.make_async_copy(qw_ref.at[heads], qw_hbm.at[heads], qw_sems.at[i]),
        ):
            store.start()
            stores.append(store)
    for store in stores:
        store.wait()


def total_kernel(r_ref, mine_ref):
    run = r_ref[0].astype(F32)
    for j in range(1, SIDE):
        run = run + r_ref[j].astype(F32)
    mine_ref[...] = run


def prefix_kernel(r_ref, p_ref):
    run = jnp.zeros((PER * DH, DH), F32)
    for j in range(SIDE):
        p_ref[j] = run.astype(BF)
        run = run + r_ref[j].astype(F32)


def pair_kernel(mine_ref, other_ref, total_ref, sent_ref):
    total = mine_ref[...] + other_ref[...]
    total_ref[...] = total
    sent_ref[...] = total.astype(BF)


def on(flag, value):
    return (value * jnp.where(flag, 1.0, 0.0)).astype(BF)


def put(out_ref, l, count, value):
    for i in range(PER):
        at = (i * count + l) * DH
        out_ref[at : at + DH, :] = value[i * DH : (i + 1) * DH, :]


def near_kernel(pos_ref, mine_ref, other_ref, total_ref, a1_ref, a2_ref, a3_ref, out_ref, sum_ref, sent_ref):
    y, core = pos_ref[1], pos_ref[2]
    a1, a2, a3 = a1_ref[...].astype(F32), a2_ref[...].astype(F32), a3_ref[...].astype(F32)
    total = total_ref[...] + (a1 + a2 + a3)
    sum_ref[...] = total
    sent_ref[...] = total.astype(BF)
    two = jnp.where(y == 2, 1.0, 0.0)
    first = jnp.where(core == 0, 1.0, 0.0)
    put(out_ref, 0, NEAR, (mine_ref[...] * first + other_ref[...] * (1.0 - first)).astype(BF))
    put(out_ref, 1, NEAR, on(y % 2 == 1, a1))
    put(out_ref, 2, NEAR, on(y >= 2, a2 + a1 * two + a3 * (1.0 - two)))


def far_kernel(pos_ref, a1_ref, a2_ref, a3_ref, out_ref):
    x = pos_ref[0]
    a1, a2, a3 = a1_ref[...].astype(F32), a2_ref[...].astype(F32), a3_ref[...].astype(F32)
    two = jnp.where(x == 2, 1.0, 0.0)
    put(out_ref, 0, FAR, on(x % 2 == 1, a1))
    put(out_ref, 1, FAR, on(x >= 2, a2 + a1 * two + a3 * (1.0 - two)))


def step_kernel(order, first, pos_ref, *refs):
    refs = refs[0 if first else 1 :]
    qw_hbm, acc_hbm, p_hbm, gain_ref = refs[:4]
    count = len(order) * PER
    states = refs[4 : 4 + 2 * len(order)]
    out_hbm, qw_ref, acc_ref, p_ref, o_ref, sems, out_sems = refs[4 + 2 * len(order) :]
    z, core = pos_ref[3], pos_ref[2]
    heads, loads = [], []
    for i in range(count):
        owner = lax.rem(z + order[i // PER] * (2 * core - 1) + SIDE, SIDE)
        h = owner * PER + i % PER
        copies = [
            pltpu.make_async_copy(qw_hbm.at[h], qw_ref.at[i], sems.at[i, 0]),
            pltpu.make_async_copy(p_hbm.at[h], p_ref.at[i], sems.at[i, 1]),
            pltpu.make_async_copy(acc_hbm.at[:, dynamic_cols(h)], acc_ref.at[i], sems.at[i, 2]),
        ]
        for copy in copies:
            copy.start()
        heads.append(h)
        loads.append(copies)
    stores = []
    for i, h in enumerate(heads):
        for copy in loads[i]:
            copy.wait()
        total = acc_ref[i] + jnp.dot(qw_ref[i, :, :DH], p_ref[i], preferred_element_type=F32)
        at = DH
        for part in states[2 * (i // PER) : 2 * (i // PER) + 2]:
            size = part.shape[0] // PER
            rows = slice(i % PER * size, (i % PER + 1) * size)
            total = total + jnp.dot(qw_ref[i, :, at : at + size], part[rows, :], preferred_element_type=F32)
            at += size
        inv = lax.rsqrt(jnp.mean(total * total, axis=-1, keepdims=True) + EPSILON)
        o_ref[i] = (total * inv * gain_ref[pl.ds(h, 1), :]).astype(BF)
        copy = pltpu.make_async_copy(o_ref.at[i], out_hbm.at[:, dynamic_cols(h)], out_sems.at[i])
        copy.start()
        stores.append(copy)
    for copy in stores:
        copy.wait()


def shift(n, s):
    return [(i, (i + s) % n) for i in range(n)]


SWAP = shift(2, 1)
RING = [(z, (z + 1) % 8) for z in range(8)] + [(8 + z, 8 + (z + 7) % 8) for z in range(8)]


def to_others(value, axis):
    a2 = lax.ppermute(value, axis, shift(4, 2))
    a1 = lax.ppermute(value, axis, shift(4, 1))
    a3 = lax.ppermute(value, axis, shift(4, 3))
    return a1, a2, a3


def swap(value):
    return lax.ppermute(value, "core", SWAP)


def body(queries, key_vectors, value_vectors, level_codes, level_table, out_gain):
    tokens = queries.shape[0]
    whole = (tokens, HEADS * DH)
    z = lax.axis_index("z")
    core = lax.axis_index("core").astype(jnp.int32)
    pos = jnp.stack([lax.axis_index("x"), lax.axis_index("y"), core, z]).astype(jnp.int32)
    codes = lax.dynamic_slice_in_dim(level_codes.T, z * tokens, tokens, 1)
    state = (PER * DH, DH)

    queries, key_vectors, value_vectors = (in_hbm(a) for a in (queries, key_vectors, value_vectors))
    states = call(
        state_kernel, sds((HEADS, DH, DH), BF), [HBM_SPEC] * 2, (2 * tokens * HEADS * DH * DH, 3 << 20),
        scratch=[pltpu.VMEM(whole, BF), pltpu.VMEM(whole, BF), DMA((2, LOADS))],
    )(key_vectors, value_vectors)
    gathered = lax.all_to_all(states, "z", split_axis=0, concat_axis=0, tiled=True)

    eye = jnp.eye(LEVELS, dtype=BF) * jnp.where(jnp.arange(LEVELS) == 1, core, 1).astype(BF)[:, None]
    table = jnp.kron(eye, level_table)
    table = jnp.pad(table, ((0, DH - LEVELS * CODES), (0, DH - LEVELS * HEADS)))
    acc, scaled = call(
        local_kernel, (sds(whole, F32), sds((HEADS, tokens, LEVELS * DH), BF)),
        [HBM_SPEC] * 3 + [VMEM_SPEC] * 2, (4 * tokens * tokens * HEADS * DH, 12 << 20),
        out_specs=(HBM_SPEC, HBM_SPEC),
        scratch=[pltpu.VMEM(whole, BF)] * 3 + [
            pltpu.VMEM(whole, F32), pltpu.VMEM((HEADS, tokens, LEVELS * DH), BF),
            DMA((3, LOADS)), DMA((LOADS,)), DMA((LOADS,)),
        ],
    )(queries, key_vectors, value_vectors, codes, table)
    acc, scaled = in_hbm(acc), in_hbm(scaled)
    gathered, acc, scaled = lax.optimization_barrier((gathered, acc, scaled))
    acc, scaled = in_hbm(acc), in_hbm(scaled)

    chunks = gathered.reshape((SIDE,) + state)
    mine = call(total_kernel, sds(state, F32), [VMEM_SPEC], (8 * 2 * DH * DH, 1 << 20))(chunks)
    other = swap(mine)
    prefixes = call(prefix_kernel, sds((SIDE,) + state, BF), [VMEM_SPEC], (8 * 2 * DH * DH, 1 << 20))(chunks)
    prefix = lax.all_to_all(prefixes.reshape(HEADS, DH, DH), "z", split_axis=0, concat_axis=0, tiled=True)
    total, sent = call(pair_kernel, (sds(state, F32), sds(state, BF)), [VMEM_SPEC] * 2, (DH * DH, 1 << 18))(mine, other)
    around = to_others(sent, "y")
    near, _, sent = call(
        near_kernel, (sds((PER * NEAR * DH, DH), BF), sds(state, F32), sds(state, BF)), [SMEM_SPEC] + [VMEM_SPEC] * 6,
        (8 * DH * DH, 1 << 18),
    )(pos, mine, other, total, *around)
    around = to_others(sent, "x")
    far = call(
        far_kernel, sds((PER * FAR * DH, DH), BF), [SMEM_SPEC] + [VMEM_SPEC] * 3, (8 * DH * DH, 1 << 18)
    )(pos, *around)

    def reads(order, arrays, out):
        n = len(order) * PER
        return call(
            functools.partial(step_kernel, order, out is None), sds(whole, BF),
            [SMEM_SPEC] + ([] if out is None else [HBM_SPEC])
            + [HBM_SPEC] * 3 + [VMEM_SPEC] * (1 + len(arrays)),
            (12 * tokens * n * DH * DH, n << 19),
            out_specs=HBM_SPEC,
            scratch=[
                pltpu.VMEM((n, tokens, LEVELS * DH), BF), pltpu.VMEM((n, tokens, DH), F32),
                pltpu.VMEM((n, DH, DH), BF), pltpu.VMEM((n, tokens, DH), BF), DMA((n, 3)), DMA((n,)),
            ],
            alias=None if out is None else {1: 0},
        )(pos, *([] if out is None else [out]), scaled, acc, prefix, out_gain, *arrays)

    a, b = near, far
    held = [((0,), [a, b])]
    for hop in range(1, 5):
        a = lax.ppermute(a, ("core", "z"), RING)
        b = lax.ppermute(b, ("core", "z"), RING)
        held.append(((hop, -hop), [a, b, swap(a), swap(b)]) if hop < 4 else ((hop,), [a, b]))
    out = None
    for hops in ((0, 1), (2,), (3, 4)):
        order = sum((held[hop][0] for hop in hops), ())
        arrays = sum((held[hop][1] for hop in hops), [])
        out = reads(order, arrays, out)
    return out


def solution(mesh):
    grid = Mesh(mesh.devices.reshape(4, 4, 2, 8), ("x", "y", "core", "z"))
    rows = P(("x", "y", "core", "z"), None)
    in_specs = (rows, rows, rows, P(("x", "y", "core"), None), P(), P())


    return jax.shard_map(body, mesh=grid, in_specs=in_specs, out_specs=rows, check_vma=False)
```

profile of v0, /device:TPU:1, one launch (start us, length us, event | category | flops | bytes accessed | tf_op | source)
XLA Modules:
  0.0 88.3 jit_solution(11163096669798032319)
XLA Ops:
  0.0 3.0 %shard_map.64 = bf16[16,128,128]{2,1,0:T(8,128)(2,1)} custom-call(bf16[256,2048]{1,0:T(8,128)(2,1)} %k_hbm.3, bf16[256,2048]{1,0:T(8,128)(2,1)} %v_hbm.3), custom_call_target="tpu_custom_call" | custom-call | flops 134217728 | bytes 3145728 | tf_op jit(solution)/shard_map/pallas_call | solution.py:257
  3.0 9.0 %all-to-all-start = ((bf16[16,128,128]{2,1,0:T(8,128)(2,1)}), bf16[16,128,128]{2,1,0:T(8,128)(2,1)S(1)}, u32[]{:S(2)}, u32[]{:S(2)}) async-start(bf16[16,128,128]{2,1,0:T(8,128)(2,1)} %shard_map.64), calls=%async_computation | async-start | bytes 1048576 | tf_op jit(solution)/shard_map/all_to_all | solution.py:261
  12.1 0.8 broadcast_multiply_fusion
  13.1 6.7 %shard_map.65 = (f32[256,2048]{1,0:T(8,128)S(1)}, bf16[16,256,768]{2,1,0:T(8,128)(2,1)S(1)}) custom-call(bf16[256,2048]{1,0:T(8,128)(2,1)} %q_hbm.1, bf16[256,2048]{1,0:T(8,128)(2,1)} %k_hbm.3, bf16[256,2048]{1,0:T(8,128)(2,1)} %v_hbm.3, s32[6,256]{1,0:T(8,128)S(1)} %dynamic-slice_bitcast_fusion.codes_ref, bf16[128,128]{1,0:T(8,128)(2,1)S(1)} %pad.4.table_ref), custom_call_target="tpu_custom_call" | custom-call | flops 536870912 | bytes 12582912 | tf_op jit(solution)/shard_map/pallas_call | solution.py:266
  19.8 2.6 %copy-done.1 = bf16[16,256,768]{2,1,0:T(8,128)(2,1)} copy-done((bf16[16,256,768]{2,1,0:T(8,128)(2,1)}, bf16[16,256,768]{2,1,0:T(8,128)(2,1)S(1)}, u32[]{:S(2)}) %copy-start.1) | copy-done | bytes 6291480
  22.4 1.4 %copy-done.2 = f32[256,2048]{1,0:T(8,128)} copy-done((f32[256,2048]{1,0:T(8,128)}, f32[256,2048]{1,0:T(8,128)S(1)}, u32[]{:S(2)}) %copy-start.2) | copy-done | bytes 2097176
  23.8 6.2 %all-to-all-done = bf16[16,128,128]{2,1,0:T(8,128)(2,1)S(1)} async-done(((bf16[16,128,128]{2,1,0:T(8,128)(2,1)}), bf16[16,128,128]{2,1,0:T(8,128)(2,1)S(1)}, u32[]{:S(2)}, u32[]{:S(2)}) %all-to-all-start) | async-done | bytes 524320 | tf_op jit(solution)/shard_map/all_to_all | solution.py:261
  30.7 0.9 shard_map.66
  31.5 3.5 %all-to-all-start.1 = ((bf16[16,128,128]{2,1,0:T(8,128)(2,1)}), bf16[16,128,128]{2,1,0:T(8,128)(2,1)S(1)}, u32[]{:S(2)}, u32[]{:S(2)}) async-start(bf16[16,128,128]{2,1,0:T(8,128)(2,1)} %bitcast.6), calls=%async_computation.1 | async-start | bytes 1048576 | tf_op jit(solution)/shard_map/all_to_all | solution.py:283
  35.1 1.4 %collective-permute-start.1 = (bf16[256,128]{1,0:T(8,128)(2,1)S(1)}, bf16[256,128]{1,0:T(8,128)(2,1)S(1)}, u32[]{:S(2)}, u32[]{:S(2)}) collective-permute-start(bf16[256,128]{1,0:T(8,128)(2,1)S(1)} %get-tuple-element.20), channel_id=1, source_target_pairs={{0,16},{16,32},{32,48},{48,0},{1,17},{17,33},{33,49},{49,1},{2,18}... | collective-permute-start | bytes 196616 | tf_op jit(solution)/shard_map/ppermute | solution.py:238
  36.5 2.6 %collective-permute-start.2 = (bf16[256,128]{1,0:T(8,128)(2,1)S(1)}, bf16[256,128]{1,0:T(8,128)(2,1)S(1)}, u32[]{:S(2)}, u32[]{:S(2)}) collective-permute-start(bf16[256,128]{1,0:T(8,128)(2,1)S(1)} %get-tuple-element.20), channel_id=1, source_target_pairs={{0,32},{16,48},{32,0},{48,16},{1,33},{17,49},{33,1},{49,17},{2,34}... | collective-permute-start | bytes 196616 | tf_op jit(solution)/shard_map/ppermute | solution.py:237
  39.1 1.1 %collective-permute-start.3 = (bf16[256,128]{1,0:T(8,128)(2,1)S(1)}, bf16[256,128]{1,0:T(8,128)(2,1)S(1)}, u32[]{:S(2)}, u32[]{:S(2)}) collective-permute-start(bf16[256,128]{1,0:T(8,128)(2,1)S(1)} %get-tuple-element.20), channel_id=1, source_target_pairs={{0,48},{16,0},{32,16},{48,32},{1,49},{17,1},{33,17},{49,33},{2,50}... | collective-permute-start | bytes 196616 | tf_op jit(solution)/shard_map/ppermute | solution.py:239
  40.2 2.4 %collective-permute-done.2.a2_ref = bf16[256,128]{1,0:T(8,128)(2,1)S(1)} collective-permute-done((bf16[256,128]{1,0:T(8,128)(2,1)S(1)}, bf16[256,128]{1,0:T(8,128)(2,1)S(1)}, u32[]{:S(2)}, u32[]{:S(2)}) %collective-permute-start.2) | collective-permute-done | bytes 65568 | tf_op jit(solution)/shard_map/ppermute | solution.py:237
  42.7 1.2 %shard_map.69 = (bf16[768,128]{1,0:T(8,128)(2,1)S(1)}, f32[256,128]{1,0:T(8,128)}, bf16[256,128]{1,0:T(8,128)(2,1)S(1)}) custom-call(s32[4]{0:T(128)S(1)} %pad_add_fusion.pos_ref, f32[256,128]{1,0:T(8,128)S(1)} %shard_map.67.mine_ref, f32[256,128]{1,0:T(8,128)S(1)} %collective-permute-done.other_ref, f32[256,128]{1,0:T(8,128)S(1)} %get-tuple-element.19.total_ref, ...), custom_call_target="tpu_custom_call" | custom-call | flops 131072 | bytes 262144 | tf_op jit(solution)/shard_map/pallas_call | solution.py:286
  43.9 2.4 %collective-permute-start.7 = (bf16[768,128]{1,0:T(8,128)(2,1)S(1)}, bf16[768,128]{1,0:T(8,128)(2,1)S(1)}, u32[]{:S(2)}, u32[]{:S(2)}) collective-permute-start(bf16[768,128]{1,0:T(8,128)(2,1)S(1)} %get-tuple-element.21.refs_4_), channel_id=1, source_target_pairs={{0,1},{1,2},{2,3},{3,4},{4,5},{5,6},{6,7},{7,0},{8,15},{9,8},{10,9... | collective-permute-start | bytes 589832 | tf_op jit(solution)/shard_map/ppermute | solution.py:313
  46.3 1.2 %collective-permute-start.4 = (bf16[256,128]{1,0:T(8,128)(2,1)S(1)}, bf16[256,128]{1,0:T(8,128)(2,1)S(1)}, u32[]{:S(2)}, u32[]{:S(2)}) collective-permute-start(bf16[256,128]{1,0:T(8,128)(2,1)S(1)} %get-tuple-element.22), channel_id=1, source_target_pairs={{0,64},{64,128},{128,192},{192,0},{1,65},{65,129},{129,193},{193,1... | collective-permute-start | bytes 196616 | tf_op jit(solution)/shard_map/ppermute | solution.py:238
  47.5 2.5 %collective-permute-start.5 = (bf16[256,128]{1,0:T(8,128)(2,1)S(1)}, bf16[256,128]{1,0:T(8,128)(2,1)S(1)}, u32[]{:S(2)}, u32[]{:S(2)}) collective-permute-start(bf16[256,128]{1,0:T(8,128)(2,1)S(1)} %get-tuple-element.22), channel_id=1, source_target_pairs={{0,128},{64,192},{128,0},{192,64},{1,129},{65,193},{129,1},{193,65... | collective-permute-start | bytes 196616 | tf_op jit(solution)/shard_map/ppermute | solution.py:237
  50.0 1.2 %collective-permute-start.6 = (bf16[256,128]{1,0:T(8,128)(2,1)S(1)}, bf16[256,128]{1,0:T(8,128)(2,1)S(1)}, u32[]{:S(2)}, u32[]{:S(2)}) collective-permute-start(bf16[256,128]{1,0:T(8,128)(2,1)S(1)} %get-tuple-element.22), channel_id=1, source_target_pairs={{0,192},{64,0},{128,64},{192,128},{1,193},{65,1},{129,65},{193,129... | collective-permute-start | bytes 196616 | tf_op jit(solution)/shard_map/ppermute | solution.py:239
  51.2 2.1 %collective-permute-start.11 = (bf16[768,128]{1,0:T(8,128)(2,1)S(1)}, bf16[768,128]{1,0:T(8,128)(2,1)S(1)}, u32[]{:S(2)}, u32[]{:S(2)}) collective-permute-start(bf16[768,128]{1,0:T(8,128)(2,1)S(1)} %collective-permute-done.7.refs_6_), channel_id=1, source_target_pairs={{0,1},{1,2},{2,3},{3,4},{4,5},{5,6},{6,7},{7,0},{8,15},{9,8},{10,9... | collective-permute-start | bytes 589832 | tf_op jit(solution)/shard_map/ppermute | solution.py:313
  54.3 1.1 %collective-permute-start.8 = (bf16[512,128]{1,0:T(8,128)(2,1)S(1)}, bf16[512,128]{1,0:T(8,128)(2,1)S(1)}, u32[]{:S(2)}, u32[]{:S(2)}) collective-permute-start(bf16[512,128]{1,0:T(8,128)(2,1)S(1)} %shard_map.70.refs_5_), channel_id=1, source_target_pairs={{0,1},{1,2},{2,3},{3,4},{4,5},{5,6},{6,7},{7,0},{8,15},{9,8},{10,9... | collective-permute-start | bytes 393224 | tf_op jit(solution)/shard_map/ppermute | solution.py:314
  55.4 3.1 %collective-permute-done.8.refs_7_ = bf16[512,128]{1,0:T(8,128)(2,1)S(1)} collective-permute-done((bf16[512,128]{1,0:T(8,128)(2,1)S(1)}, bf16[512,128]{1,0:T(8,128)(2,1)S(1)}, u32[]{:S(2)}, u32[]{:S(2)}) %collective-permute-start.8) | collective-permute-done | bytes 131104 | tf_op jit(solution)/shard_map/ppermute | solution.py:314
  58.5 2.0 %collective-permute-start.12 = (bf16[512,128]{1,0:T(8,128)(2,1)S(1)}, bf16[512,128]{1,0:T(8,128)(2,1)S(1)}, u32[]{:S(2)}, u32[]{:S(2)}) collective-permute-start(bf16[512,128]{1,0:T(8,128)(2,1)S(1)} %collective-permute-done.8.refs_7_), channel_id=1, source_target_pairs={{0,1},{1,2},{2,3},{3,4},{4,5},{5,6},{6,7},{7,0},{8,15},{9,8},{10,9... | collective-permute-start | bytes 393224 | tf_op jit(solution)/shard_map/ppermute | solution.py:314
  60.5 0.7 collective-permute-start.15
  61.2 3.2 %collective-permute-start.9 = (bf16[768,128]{1,0:T(8,128)(2,1)S(1)}, bf16[768,128]{1,0:T(8,128)(2,1)S(1)}, u32[]{:S(2)}, u32[]{:S(2)}) collective-permute-start(bf16[768,128]{1,0:T(8,128)(2,1)S(1)} %collective-permute-done.7.refs_6_), channel_id=1, source_target_pairs={{0,8},{8,0},{1,9},{9,1},{2,10},{10,2},{3,11},{11,3},{4,12},{12,4},... | collective-permute-start | bytes 589832 | tf_op jit(solution)/shard_map/ppermute | solution.py:244
  64.4 1.3 %collective-permute-start.16 = (bf16[512,128]{1,0:T(8,128)(2,1)S(1)}, bf16[512,128]{1,0:T(8,128)(2,1)S(1)}, u32[]{:S(2)}, u32[]{:S(2)}) collective-permute-start(bf16[512,128]{1,0:T(8,128)(2,1)S(1)} %collective-permute-done.12.refs_6_), channel_id=1, source_target_pairs={{0,1},{1,2},{2,3},{3,4},{4,5},{5,6},{6,7},{7,0},{8,15},{9,8},{10,9... | collective-permute-start | bytes 393224 | tf_op jit(solution)/shard_map/ppermute | solution.py:314
  65.6 3.0 %collective-permute-start.14 = (bf16[512,128]{1,0:T(8,128)(2,1)S(1)}, bf16[512,128]{1,0:T(8,128)(2,1)S(1)}, u32[]{:S(2)}, u32[]{:S(2)}) collective-permute-start(bf16[512,128]{1,0:T(8,128)(2,1)S(1)} %collective-permute-done.12.refs_6_), channel_id=1, source_target_pairs={{0,8},{8,0},{1,9},{9,1},{2,10},{10,2},{3,11},{11,3},{4,12},{12,4},... | collective-permute-start | bytes 393224 | tf_op jit(solution)/shard_map/ppermute | solution.py:244
  68.7 2.0 %collective-permute-start.17 = (bf16[768,128]{1,0:T(8,128)(2,1)S(1)}, bf16[768,128]{1,0:T(8,128)(2,1)S(1)}, u32[]{:S(2)}, u32[]{:S(2)}) collective-permute-start(bf16[768,128]{1,0:T(8,128)(2,1)S(1)} %collective-permute-done.15.refs_5_), channel_id=1, source_target_pairs={{0,8},{8,0},{1,9},{9,1},{2,10},{10,2},{3,11},{11,3},{4,12},{12,4},... | collective-permute-start | bytes 589832 | tf_op jit(solution)/shard_map/ppermute | solution.py:244
  70.7 1.4 %collective-permute-start.19 = (bf16[768,128]{1,0:T(8,128)(2,1)S(1)}, bf16[768,128]{1,0:T(8,128)(2,1)S(1)}, u32[]{:S(2)}, u32[]{:S(2)}) collective-permute-start(bf16[768,128]{1,0:T(8,128)(2,1)S(1)} %collective-permute-done.15.refs_5_), channel_id=1, source_target_pairs={{0,1},{1,2},{2,3},{3,4},{4,5},{5,6},{6,7},{7,0},{8,15},{9,8},{10,9... | collective-permute-start | bytes 589832 | tf_op jit(solution)/shard_map/ppermute | solution.py:313
  72.1 2.7 %collective-permute-start.18 = (bf16[512,128]{1,0:T(8,128)(2,1)S(1)}, bf16[512,128]{1,0:T(8,128)(2,1)S(1)}, u32[]{:S(2)}, u32[]{:S(2)}) collective-permute-start(bf16[512,128]{1,0:T(8,128)(2,1)S(1)} %collective-permute-done.16.refs_6_), channel_id=1, source_target_pairs={{0,8},{8,0},{1,9},{9,1},{2,10},{10,2},{3,11},{11,3},{4,12},{12,4},... | collective-permute-start | bytes 393224 | tf_op jit(solution)/shard_map/ppermute | solution.py:244
  74.8 4.7 %shard_map.71.refs_0_ = bf16[256,2048]{1,0:T(8,128)(2,1)} custom-call(s32[4]{0:T(128)S(1)} %pad_add_fusion.pos_ref, bf16[16,256,768]{2,1,0:T(8,128)(2,1)} %copy-done.1, f32[256,2048]{1,0:T(8,128)} %copy-done.2, bf16[16,128,128]{2,1,0:T(8,128)(2,1)S(1)} %all-to-all-done.1.refs_2_.refs_3_, f32[16,128]{1,0:T(8,128)S(1)} %copy-done.3, ...), custom_call_target="tpu_custom_call" | custom-call | flops 301989888 | bytes 3145728 | tf_op jit(solution)/shard_map/pallas_call | solution.py:297
  79.5 3.9 %shard_map.72.refs_0_ = bf16[256,2048]{1,0:T(8,128)(2,1)} custom-call(s32[4]{0:T(128)S(1)} %pad_add_fusion.pos_ref, bf16[256,2048]{1,0:T(8,128)(2,1)} %shard_map.71.refs_0_, bf16[16,256,768]{2,1,0:T(8,128)(2,1)} %copy-done.1, f32[256,2048]{1,0:T(8,128)} %copy-done.2, ...), custom_call_target="tpu_custom_call", output_to_operand_aliasing={{}: (1, {})} | custom-call | flops 201326592 | bytes 2097152 | tf_op jit(solution)/shard_map/pallas_call | solution.py:297
  83.4 4.7 %shard_map.73 = bf16[256,2048]{1,0:T(8,128)(2,1)} custom-call(s32[4]{0:T(128)S(1)} %pad_add_fusion.pos_ref, bf16[256,2048]{1,0:T(8,128)(2,1)} %shard_map.72.refs_0_, bf16[16,256,768]{2,1,0:T(8,128)(2,1)} %copy-done.1, f32[256,2048]{1,0:T(8,128)} %copy-done.2, ...), custom_call_target="tpu_custom_call", output_to_operand_aliasing={{}: (1, {})} | custom-call | flops 301989888 | bytes 3145728 | tf_op jit(solution)/shard_map/pallas_call | solution.py:297
  (39 shorter events, 2.2 us)
Async XLA Ops:
  0.0 13.1 %copy-start = (s32[2048,6]{0,1:T(8,128)S(1)}, s32[2048,6]{0,1:T(8,128)}, u32[]{:S(2)}) copy-start(s32[2048,6]{0,1:T(8,128)} %param.9) | copy-start | bytes 147460
  0.0 74.8 %copy-start.3 = (f32[16,128]{1,0:T(8,128)S(1)}, f32[16,128]{1,0:T(8,128)}, u32[]{:S(2)}) copy-start(f32[16,128]{1,0:T(8,128)} %refs_4_.3) | copy-start | bytes 24580
  3.0 27.0 %all-to-all-start = ((bf16[16,128,128]{2,1,0:T(8,128)(2,1)}), bf16[16,128,128]{2,1,0:T(8,128)(2,1)S(1)}, u32[]{:S(2)}, u32[]{:S(2)}) async-start(bf16[16,128,128]{2,1,0:T(8,128)(2,1)} %shard_map.64), calls=%async_computation | async-start | bytes 1048576 | tf_op jit(solution)/shard_map/all_to_all | solution.py:261
  19.8 2.6 %copy-start.1 = (bf16[16,256,768]{2,1,0:T(8,128)(2,1)}, bf16[16,256,768]{2,1,0:T(8,128)(2,1)S(1)}, u32[]{:S(2)}) copy-start(bf16[16,256,768]{2,1,0:T(8,128)(2,1)S(1)} %get-tuple-element.16.refs_0_.refs_1_) | copy-start | bytes 18874372
  22.4 1.4 %copy-start.2 = (f32[256,2048]{1,0:T(8,128)}, f32[256,2048]{1,0:T(8,128)S(1)}, u32[]{:S(2)}) copy-start(f32[256,2048]{1,0:T(8,128)S(1)} %get-tuple-element.17.refs_1_.refs_2_) | copy-start | bytes 6291460
  30.1 5.0 %collective-permute-start = (f32[256,128]{1,0:T(8,128)S(1)}, f32[256,128]{1,0:T(8,128)S(1)}, u32[]{:S(2)}, u32[]{:S(2)}) collective-permute-start(f32[256,128]{1,0:T(8,128)S(1)} %shard_map.67.mine_ref), channel_id=1, source_target_pairs={{0,8},{8,0},{1,9},{9,1},{2,10},{10,2},{3,11},{11,3},{4,12},{12,4},... | collective-permute-start | bytes 393224 | tf_op jit(solution)/shard_map/ppermute | solution.py:244
  31.5 43.2 %all-to-all-start.1 = ((bf16[16,128,128]{2,1,0:T(8,128)(2,1)}), bf16[16,128,128]{2,1,0:T(8,128)(2,1)S(1)}, u32[]{:S(2)}, u32[]{:S(2)}) async-start(bf16[16,128,128]{2,1,0:T(8,128)(2,1)} %bitcast.6), calls=%async_computation.1 | async-start | bytes 1048576 | tf_op jit(solution)/shard_map/all_to_all | solution.py:283
  35.1 5.1 %collective-permute-start.1 = (bf16[256,128]{1,0:T(8,128)(2,1)S(1)}, bf16[256,128]{1,0:T(8,128)(2,1)S(1)}, u32[]{:S(2)}, u32[]{:S(2)}) collective-permute-start(bf16[256,128]{1,0:T(8,128)(2,1)S(1)} %get-tuple-element.20), channel_id=1, source_target_pairs={{0,16},{16,32},{32,48},{48,0},{1,17},{17,33},{33,49},{49,1},{2,18}... | collective-permute-start | bytes 196616 | tf_op jit(solution)/shard_map/ppermute | solution.py:238
  36.5 6.2 %collective-permute-start.2 = (bf16[256,128]{1,0:T(8,128)(2,1)S(1)}, bf16[256,128]{1,0:T(8,128)(2,1)S(1)}, u32[]{:S(2)}, u32[]{:S(2)}) collective-permute-start(bf16[256,128]{1,0:T(8,128)(2,1)S(1)} %get-tuple-element.20), channel_id=1, source_target_pairs={{0,32},{16,48},{32,0},{48,16},{1,33},{17,49},{33,1},{49,17},{2,34}... | collective-permute-start | bytes 196616 | tf_op jit(solution)/shard_map/ppermute | solution.py:237
  39.1 3.6 %collective-permute-start.3 = (bf16[256,128]{1,0:T(8,128)(2,1)S(1)}, bf16[256,128]{1,0:T(8,128)(2,1)S(1)}, u32[]{:S(2)}, u32[]{:S(2)}) collective-permute-start(bf16[256,128]{1,0:T(8,128)(2,1)S(1)} %get-tuple-element.20), channel_id=1, source_target_pairs={{0,48},{16,0},{32,16},{48,32},{1,49},{17,1},{33,17},{49,33},{2,50}... | collective-permute-start | bytes 196616 | tf_op jit(solution)/shard_map/ppermute | solution.py:239
  43.9 7.3 %collective-permute-start.7 = (bf16[768,128]{1,0:T(8,128)(2,1)S(1)}, bf16[768,128]{1,0:T(8,128)(2,1)S(1)}, u32[]{:S(2)}, u32[]{:S(2)}) collective-permute-start(bf16[768,128]{1,0:T(8,128)(2,1)S(1)} %get-tuple-element.21.refs_4_), channel_id=1, source_target_pairs={{0,1},{1,2},{2,3},{3,4},{4,5},{5,6},{6,7},{7,0},{8,15},{9,8},{10,9... | collective-permute-start | bytes 589832 | tf_op jit(solution)/shard_map/ppermute | solution.py:313
  46.3 7.0 %collective-permute-start.4 = (bf16[256,128]{1,0:T(8,128)(2,1)S(1)}, bf16[256,128]{1,0:T(8,128)(2,1)S(1)}, u32[]{:S(2)}, u32[]{:S(2)}) collective-permute-start(bf16[256,128]{1,0:T(8,128)(2,1)S(1)} %get-tuple-element.22), channel_id=1, source_target_pairs={{0,64},{64,128},{128,192},{192,0},{1,65},{65,129},{129,193},{193,1... | collective-permute-start | bytes 196616 | tf_op jit(solution)/shard_map/ppermute | solution.py:238
  47.5 5.8 %collective-permute-start.5 = (bf16[256,128]{1,0:T(8,128)(2,1)S(1)}, bf16[256,128]{1,0:T(8,128)(2,1)S(1)}, u32[]{:S(2)}, u32[]{:S(2)}) collective-permute-start(bf16[256,128]{1,0:T(8,128)(2,1)S(1)} %get-tuple-element.22), channel_id=1, source_target_pairs={{0,128},{64,192},{128,0},{192,64},{1,129},{65,193},{129,1},{193,65... | collective-permute-start | bytes 196616 | tf_op jit(solution)/shard_map/ppermute | solution.py:237
  50.0 3.7 %collective-permute-start.6 = (bf16[256,128]{1,0:T(8,128)(2,1)S(1)}, bf16[256,128]{1,0:T(8,128)(2,1)S(1)}, u32[]{:S(2)}, u32[]{:S(2)}) collective-permute-start(bf16[256,128]{1,0:T(8,128)(2,1)S(1)} %get-tuple-element.22), channel_id=1, source_target_pairs={{0,192},{64,0},{128,64},{192,128},{1,193},{65,1},{129,65},{193,129... | collective-permute-start | bytes 196616 | tf_op jit(solution)/shard_map/ppermute | solution.py:239
  51.2 9.3 %collective-permute-start.11 = (bf16[768,128]{1,0:T(8,128)(2,1)S(1)}, bf16[768,128]{1,0:T(8,128)(2,1)S(1)}, u32[]{:S(2)}, u32[]{:S(2)}) collective-permute-start(bf16[768,128]{1,0:T(8,128)(2,1)S(1)} %collective-permute-done.7.refs_6_), channel_id=1, source_target_pairs={{0,1},{1,2},{2,3},{3,4},{4,5},{5,6},{6,7},{7,0},{8,15},{9,8},{10,9... | collective-permute-start | bytes 589832 | tf_op jit(solution)/shard_map/ppermute | solution.py:313
  54.3 4.2 %collective-permute-start.8 = (bf16[512,128]{1,0:T(8,128)(2,1)S(1)}, bf16[512,128]{1,0:T(8,128)(2,1)S(1)}, u32[]{:S(2)}, u32[]{:S(2)}) collective-permute-start(bf16[512,128]{1,0:T(8,128)(2,1)S(1)} %shard_map.70.refs_5_), channel_id=1, source_target_pairs={{0,1},{1,2},{2,3},{3,4},{4,5},{5,6},{6,7},{7,0},{8,15},{9,8},{10,9... | collective-permute-start | bytes 393224 | tf_op jit(solution)/shard_map/ppermute | solution.py:314
  58.5 5.9 %collective-permute-start.12 = (bf16[512,128]{1,0:T(8,128)(2,1)S(1)}, bf16[512,128]{1,0:T(8,128)(2,1)S(1)}, u32[]{:S(2)}, u32[]{:S(2)}) collective-permute-start(bf16[512,128]{1,0:T(8,128)(2,1)S(1)} %collective-permute-done.8.refs_7_), channel_id=1, source_target_pairs={{0,1},{1,2},{2,3},{3,4},{4,5},{5,6},{6,7},{7,0},{8,15},{9,8},{10,9... | collective-permute-start | bytes 393224 | tf_op jit(solution)/shard_map/ppermute | solution.py:314
  60.5 8.2 %collective-permute-start.15 = (bf16[768,128]{1,0:T(8,128)(2,1)S(1)}, bf16[768,128]{1,0:T(8,128)(2,1)S(1)}, u32[]{:S(2)}, u32[]{:S(2)}) collective-permute-start(bf16[768,128]{1,0:T(8,128)(2,1)S(1)} %collective-permute-done.11.refs_5_), channel_id=1, source_target_pairs={{0,1},{1,2},{2,3},{3,4},{4,5},{5,6},{6,7},{7,0},{8,15},{9,8},{10,9... | collective-permute-start | bytes 589832 | tf_op jit(solution)/shard_map/ppermute | solution.py:313
  61.2 9.5 %collective-permute-start.9 = (bf16[768,128]{1,0:T(8,128)(2,1)S(1)}, bf16[768,128]{1,0:T(8,128)(2,1)S(1)}, u32[]{:S(2)}, u32[]{:S(2)}) collective-permute-start(bf16[768,128]{1,0:T(8,128)(2,1)S(1)} %collective-permute-done.7.refs_6_), channel_id=1, source_target_pairs={{0,8},{8,0},{1,9},{9,1},{2,10},{10,2},{3,11},{11,3},{4,12},{12,4},... | collective-permute-start | bytes 589832 | tf_op jit(solution)/shard_map/ppermute | solution.py:244
  64.4 4.2 %collective-permute-start.10 = (bf16[512,128]{1,0:T(8,128)(2,1)S(1)}, bf16[512,128]{1,0:T(8,128)(2,1)S(1)}, u32[]{:S(2)}, u32[]{:S(2)}) collective-permute-start(bf16[512,128]{1,0:T(8,128)(2,1)S(1)} %collective-permute-done.8.refs_7_), channel_id=1, source_target_pairs={{0,8},{8,0},{1,9},{9,1},{2,10},{10,2},{3,11},{11,3},{4,12},{12,4},... | collective-permute-start | bytes 393224 | tf_op jit(solution)/shard_map/ppermute | solution.py:244
  64.4 7.7 %collective-permute-start.16 = (bf16[512,128]{1,0:T(8,128)(2,1)S(1)}, bf16[512,128]{1,0:T(8,128)(2,1)S(1)}, u32[]{:S(2)}, u32[]{:S(2)}) collective-permute-start(bf16[512,128]{1,0:T(8,128)(2,1)S(1)} %collective-permute-done.12.refs_6_), channel_id=1, source_target_pairs={{0,1},{1,2},{2,3},{3,4},{4,5},{5,6},{6,7},{7,0},{8,15},{9,8},{10,9... | collective-permute-start | bytes 393224 | tf_op jit(solution)/shard_map/ppermute | solution.py:314
  65.6 9.1 %collective-permute-start.14 = (bf16[512,128]{1,0:T(8,128)(2,1)S(1)}, bf16[512,128]{1,0:T(8,128)(2,1)S(1)}, u32[]{:S(2)}, u32[]{:S(2)}) collective-permute-start(bf16[512,128]{1,0:T(8,128)(2,1)S(1)} %collective-permute-done.12.refs_6_), channel_id=1, source_target_pairs={{0,8},{8,0},{1,9},{9,1},{2,10},{10,2},{3,11},{11,3},{4,12},{12,4},... | collective-permute-start | bytes 393224 | tf_op jit(solution)/shard_map/ppermute | solution.py:244
  68.6 10.9 %collective-permute-start.13 = (bf16[768,128]{1,0:T(8,128)(2,1)S(1)}, bf16[768,128]{1,0:T(8,128)(2,1)S(1)}, u32[]{:S(2)}, u32[]{:S(2)}) collective-permute-start(bf16[768,128]{1,0:T(8,128)(2,1)S(1)} %collective-permute-done.11.refs_5_), channel_id=1, source_target_pairs={{0,8},{8,0},{1,9},{9,1},{2,10},{10,2},{3,11},{11,3},{4,12},{12,4},... | collective-permute-start | bytes 589832 | tf_op jit(solution)/shard_map/ppermute | solution.py:244
  68.7 14.7 %collective-permute-start.17 = (bf16[768,128]{1,0:T(8,128)(2,1)S(1)}, bf16[768,128]{1,0:T(8,128)(2,1)S(1)}, u32[]{:S(2)}, u32[]{:S(2)}) collective-permute-start(bf16[768,128]{1,0:T(8,128)(2,1)S(1)} %collective-permute-done.15.refs_5_), channel_id=1, source_target_pairs={{0,8},{8,0},{1,9},{9,1},{2,10},{10,2},{3,11},{11,3},{4,12},{12,4},... | collective-permute-start | bytes 589832 | tf_op jit(solution)/shard_map/ppermute | solution.py:244
  70.7 12.7 %collective-permute-start.19 = (bf16[768,128]{1,0:T(8,128)(2,1)S(1)}, bf16[768,128]{1,0:T(8,128)(2,1)S(1)}, u32[]{:S(2)}, u32[]{:S(2)}) collective-permute-start(bf16[768,128]{1,0:T(8,128)(2,1)S(1)} %collective-permute-done.15.refs_5_), channel_id=1, source_target_pairs={{0,1},{1,2},{2,3},{3,4},{4,5},{5,6},{6,7},{7,0},{8,15},{9,8},{10,9... | collective-permute-start | bytes 589832 | tf_op jit(solution)/shard_map/ppermute | solution.py:313
  72.1 11.3 %collective-permute-start.18 = (bf16[512,128]{1,0:T(8,128)(2,1)S(1)}, bf16[512,128]{1,0:T(8,128)(2,1)S(1)}, u32[]{:S(2)}, u32[]{:S(2)}) collective-permute-start(bf16[512,128]{1,0:T(8,128)(2,1)S(1)} %collective-permute-done.16.refs_6_), channel_id=1, source_target_pairs={{0,8},{8,0},{1,9},{9,1},{2,10},{10,2},{3,11},{11,3},{4,12},{12,4},... | collective-permute-start | bytes 393224 | tf_op jit(solution)/shard_map/ppermute | solution.py:244
  74.8 8.6 %collective-permute-start.20 = (bf16[512,128]{1,0:T(8,128)(2,1)S(1)}, bf16[512,128]{1,0:T(8,128)(2,1)S(1)}, u32[]{:S(2)}, u32[]{:S(2)}) collective-permute-start(bf16[512,128]{1,0:T(8,128)(2,1)S(1)} %collective-permute-done.16.refs_6_), channel_id=1, source_target_pairs={{0,1},{1,2},{2,3},{3,4},{4,5},{5,6},{6,7},{7,0},{8,15},{9,8},{10,9... | collective-permute-start | bytes 393224 | tf_op jit(solution)/shard_map/ppermute | solution.py:314
where the time goes:
time: 88.6 us; the launch traced here: 88.3 us
  starting transfers between devices  44.9 us (51%)
  Pallas kernels  25.7 us (29%)
  waiting for transfers between devices  12.2 us (14%)
  local copies, waits for them, and re-layouts  4.19 us (5%)
  other arithmetic  0.92 us (1%)
    pallas_call x3, Pallas kernels, reads(): call(functools.partial(step_kernel, order, out is None), sds(whole, BF),...  13.2 us
    ppermute x7, starting transfers between devices, swap(): return lax.ppermute(value, 'core', SWAP)  11.5 us
    all_to_all x1, starting transfers between devices, body(): lax.all_to_all(states, 'z', split_axis=0, concat_axis=0, tiled=True)  9.01 us
    pallas_call x1, Pallas kernels, body(): call(local_kernel, (sds(whole, F32), sds((HEADS, tokens, LEVELS * DH), BF...  6.68 us
    ppermute x4, starting transfers between devices, body(): a = lax.ppermute(a, ('core', 'z'), RING)  6.64 us
    all_to_all x1, waiting for transfers between devices, body(): lax.all_to_all(states, 'z', split_axis=0, concat_axis=0, tiled=True)  6.2 us
    ppermute x2, starting transfers between devices, to_others(): a2 = lax.ppermute(value, axis, shift(4, 2))  5.07 us
    ppermute x4, starting transfers between devices, body(): b = lax.ppermute(b, ('core', 'z'), RING)  4.36 us
  transfers between devices with their start and end apart: 23, of which 5 were waited for; matrix products, arithmetic and copies ran while one was open for 1% of the time, Pallas kernels for 20%

commit v1 on v0

--- a/solution.py
+++ b/solution.py
@@ -158,44 +158,56 @@
     return (value * jnp.where(flag, 1.0, 0.0)).astype(BF)
 
 
-def put(out_ref, l, count, value):
+def put(out_refs, l, value):
     for i in range(PER):
-        at = (i * count + l) * DH
-        out_ref[at : at + DH, :] = value[i * DH : (i + 1) * DH, :]
-
-
-def near_kernel(pos_ref, mine_ref, other_ref, total_ref, a1_ref, a2_ref, a3_ref, out_ref, sum_ref, sent_ref):
+        out_refs[i][l * DH : (l + 1) * DH, :] = value[i * DH : (i + 1) * DH, :]
+
+
+def near_kernel(pos_ref, mine_ref, other_ref, total_ref, a1_ref, a2_ref, a3_ref, *outs):
     y, core = pos_ref[1], pos_ref[2]
     a1, a2, a3 = a1_ref[...].astype(F32), a2_ref[...].astype(F32), a3_ref[...].astype(F32)
-    total = total_ref[...] + (a1 + a2 + a3)
-    sum_ref[...] = total
-    sent_ref[...] = total.astype(BF)
+    outs[PER][...] = (total_ref[...] + (a1 + a2 + a3)).astype(BF)
     two = jnp.where(y == 2, 1.0, 0.0)
     first = jnp.where(core == 0, 1.0, 0.0)
-    put(out_ref, 0, NEAR, (mine_ref[...] * first + other_ref[...] * (1.0 - first)).astype(BF))
-    put(out_ref, 1, NEAR, on(y % 2 == 1, a1))
-    put(out_ref, 2, NEAR, on(y >= 2, a2 + a1 * two + a3 * (1.0 - two)))
-
-
-def far_kernel(pos_ref, a1_ref, a2_ref, a3_ref, out_ref):
+    put(outs, 0, (mine_ref[...] * first + other_ref[...] * (1.0 - first)).astype(BF))
+    put(outs, 1, on(y % 2 == 1, a1))
+    put(outs, 2, on(y >= 2, a2 + a1 * two + a3 * (1.0 - two)))
+
+
+def far_kernel(pos_ref, a1_ref, a2_ref, a3_ref, *outs):
     x = pos_ref[0]
     a1, a2, a3 = a1_ref[...].astype(F32), a2_ref[...].astype(F32), a3_ref[...].astype(F32)
     two = jnp.where(x == 2, 1.0, 0.0)
-    put(out_ref, 0, FAR, on(x % 2 == 1, a1))
-    put(out_ref, 1, FAR, on(x >= 2, a2 + a1 * two + a3 * (1.0 - two)))
+    put(outs, 0, on(x % 2 == 1, a1))
+    put(outs, 1, on(x >= 2, a2 + a1 * two + a3 * (1.0 - two)))
+
+
+def head_at(pos_ref, order, i):
+    owner = lax.rem(pos_ref[3] + order[i // PER] * (2 * pos_ref[2] - 1) + SIDE, SIDE)
+    return owner * PER + i % PER
+
+
+def finish(i, h, total, scaled, at, states, gain_ref, o_ref, out_hbm, out_sems):
+    for part in states[2 * i : 2 * i + 2]:
+        size = part.shape[0]
+        total = total + jnp.dot(scaled[:, at : at + size], part[...], preferred_element_type=F32)
+        at += size
+    inv = lax.rsqrt(jnp.mean(total * total, axis=-1, keepdims=True) + EPSILON)
+    o_ref[i] = (total * inv * gain_ref[pl.ds(h, 1), :]).astype(BF)
+    copy = pltpu.make_async_copy(o_ref.at[i], out_hbm.at[:, dynamic_cols(h)], out_sems.at[i])
+    copy.start()
+    return copy
 
 
 def step_kernel(order, first, pos_ref, *refs):
     refs = refs[0 if first else 1 :]
     qw_hbm, acc_hbm, p_hbm, gain_ref = refs[:4]
     count = len(order) * PER
-    states = refs[4 : 4 + 2 * len(order)]
-    out_hbm, qw_ref, acc_ref, p_ref, o_ref, sems, out_sems = refs[4 + 2 * len(order) :]
-    z, core = pos_ref[3], pos_ref[2]
-    heads, loads = [], []
+    states = refs[4 : 4 + 2 * count]
+    out_hbm, qw_ref, acc_ref, p_ref, o_ref, sems, out_sems = refs[4 + 2 * count :]
+    loads = []
     for i in range(count):
-        owner = lax.rem(z + order[i // PER] * (2 * core - 1) + SIDE, SIDE)
-        h = owner * PER + i % PER
+        h = head_at(pos_ref, order, i)
         copies = [
             pltpu.make_async_copy(qw_hbm.at[h], qw_ref.at[i], sems.at[i, 0]),
             pltpu.make_async_copy(p_hbm.at[h], p_ref.at[i], sems.at[i, 1]),
@@ -203,24 +215,51 @@
         ]
         for copy in copies:
             copy.start()
-        heads.append(h)
         loads.append(copies)
     stores = []
-    for i, h in enumerate(heads):
+    for i in range(count):
         for copy in loads[i]:
             copy.wait()
         total = acc_ref[i] + jnp.dot(qw_ref[i, :, :DH], p_ref[i], preferred_element_type=F32)
-        at = DH
-        for part in states[2 * (i // PER) : 2 * (i // PER) + 2]:
-            size = part.shape[0] // PER
-            rows = slice(i % PER * size, (i % PER + 1) * size)
-            total = total + jnp.dot(qw_ref[i, :, at : at + size], part[rows, :], preferred_element_type=F32)
-            at += size
-        inv = lax.rsqrt(jnp.mean(total * total, axis=-1, keepdims=True) + EPSILON)
-        o_ref[i] = (total * inv * gain_ref[pl.ds(h, 1), :]).astype(BF)
-        copy = pltpu.make_async_copy(o_ref.at[i], out_hbm.at[:, dynamic_cols(h)], out_sems.at[i])
-        copy.start()
-        stores.append(copy)
+        stores.append(
+            finish(i, head_at(pos_ref, order, i), total, qw_ref.at[i], DH, states, gain_ref, o_ref, out_hbm, out_sems)
+        )
+    for copy in stores:
+        copy.wait()
+
+
+def load_kernel(order, pos_ref, qw_hbm, acc_hbm, p_hbm, qw_out, acc_out, q_ref, p_ref, sems):
+    count = len(order) * PER
+    loads = []
+    for i in range(count):
+        h = head_at(pos_ref, order, i)
+        copies = [
+            pltpu.make_async_copy(qw_hbm.at[h, :, pl.ds(0, DH)], q_ref.at[i], sems.at[i, 0]),
+            pltpu.make_async_copy(p_hbm.at[h], p_ref.at[i], sems.at[i, 1]),
+            pltpu.make_async_copy(acc_hbm.at[:, dynamic_cols(h)], acc_out.at[i], sems.at[i, 2]),
+            pltpu.make_async_copy(qw_hbm.at[h, :, pl.ds(DH, (LEVELS - 1) * DH)], qw_out.at[i], sems.at[i, 3]),
+        ]
+        for copy in copies:
+            copy.start()
+        loads.append(copies)
+    for i in range(count):
+        for copy in loads[i][:3]:
+            copy.wait()
+        acc_out[i] = acc_out[i] + jnp.dot(q_ref[i], p_ref[i], preferred_element_type=F32)
+    for copies in loads:
+        copies[3].wait()
+
+
+def last_kernel(order, pos_ref, prev_hbm, qw_ref, acc_ref, gain_ref, *refs):
+    count = len(order) * PER
+    states = refs[: 2 * count]
+    out_hbm, o_ref, out_sems = refs[2 * count :]
+    stores = [
+        finish(
+            i, head_at(pos_ref, order, i), acc_ref[i], qw_ref.at[i], 0, states, gain_ref, o_ref, out_hbm, out_sems
+        )
+        for i in range(count)
+    ]
     for copy in stores:
         copy.wait()
 
@@ -283,21 +322,34 @@
     prefix = lax.all_to_all(prefixes.reshape(HEADS, DH, DH), "z", split_axis=0, concat_axis=0, tiled=True)
     total, sent = call(pair_kernel, (sds(state, F32), sds(state, BF)), [VMEM_SPEC] * 2, (DH * DH, 1 << 18))(mine, other)
     around = to_others(sent, "y")
-    near, _, sent = call(
-        near_kernel, (sds((PER * NEAR * DH, DH), BF), sds(state, F32), sds(state, BF)), [SMEM_SPEC] + [VMEM_SPEC] * 6,
+    *near, sent = call(
+        near_kernel, (sds((NEAR * DH, DH), BF),) * PER + (sds(state, BF),), [SMEM_SPEC] + [VMEM_SPEC] * 6,
         (8 * DH * DH, 1 << 18),
     )(pos, mine, other, total, *around)
     around = to_others(sent, "x")
     far = call(
-        far_kernel, sds((PER * FAR * DH, DH), BF), [SMEM_SPEC] + [VMEM_SPEC] * 3, (8 * DH * DH, 1 << 18)
+        far_kernel, (sds((FAR * DH, DH), BF),) * PER, [SMEM_SPEC] + [VMEM_SPEC] * 3, (8 * DH * DH, 1 << 18)
     )(pos, *around)
 
-    def reads(order, arrays, out):
+    near, far = list(near), list(far)
+
+    def paired():
+        return [part[i] for i in range(PER) for part in (near, far)]
+
+    held = [((0,), paired())]
+    for hop in range(1, 5):
+        near = [lax.ppermute(part, ("core", "z"), RING) for part in near]
+        far = [lax.ppermute(part, ("core", "z"), RING) for part in far]
+        arrays = paired()
+        held.append(((hop, -hop), arrays + [swap(a) for a in arrays]) if hop < 4 else ((hop,), arrays))
+
+    out = None
+    for hop in range(2):
+        order, arrays = held[hop]
         n = len(order) * PER
-        return call(
+        out = call(
             functools.partial(step_kernel, order, out is None), sds(whole, BF),
-            [SMEM_SPEC] + ([] if out is None else [HBM_SPEC])
-            + [HBM_SPEC] * 3 + [VMEM_SPEC] * (1 + len(arrays)),
+            [SMEM_SPEC] + ([] if out is None else [HBM_SPEC]) + [HBM_SPEC] * 3 + [VMEM_SPEC] * (1 + len(arrays)),
             (12 * tokens * n * DH * DH, n << 19),
             out_specs=HBM_SPEC,
             scratch=[
@@ -306,19 +358,20 @@
             ],
             alias=None if out is None else {1: 0},
         )(pos, *([] if out is None else [out]), scaled, acc, prefix, out_gain, *arrays)
-
-    a, b = near, far
-    held = [((0,), [a, b])]
-    for hop in range(1, 5):
-        a = lax.ppermute(a, ("core", "z"), RING)
-        b = lax.ppermute(b, ("core", "z"), RING)
-        held.append(((hop, -hop), [a, b, swap(a), swap(b)]) if hop < 4 else ((hop,), [a, b]))
-    out = None
-    for hops in ((0, 1), (2,), (3, 4)):
-        order = sum((held[hop][0] for hop in hops), ())
-        arrays = sum((held[hop][1] for hop in hops), [])
-        out = reads(order, arrays, out)
-    return out
+    order = sum((held[hop][0] for hop in (2, 3, 4)), ())
+    arrays = sum((held[hop][1] for hop in (2, 3, 4)), [])
+    n = len(order) * PER
+    scaled, acc = call(
+        functools.partial(load_kernel, order),
+        (sds((n, tokens, (LEVELS - 1) * DH), BF), sds((n, tokens, DH), F32)),
+        [SMEM_SPEC] + [HBM_SPEC] * 3, (2 * tokens * n * DH * DH, n << 19),
+        scratch=[pltpu.VMEM((n, tokens, DH), BF), pltpu.VMEM((n, DH, DH), BF), DMA((n, 4))],
+    )(pos, scaled, acc, prefix)
+    return call(
+        functools.partial(last_kernel, order), sds(whole, BF),
+        [SMEM_SPEC, HBM_SPEC] + [VMEM_SPEC] * (3 + len(arrays)), (10 * tokens * n * DH * DH, n << 19),
+        out_specs=HBM_SPEC, scratch=[pltpu.VMEM((n, tokens, DH), BF), DMA((n,))], alias={1: 0},
+    )(pos, out, scaled, acc, out_gain, *arrays)
 
 
 def solution(mesh):
@@ -326,5 +379,4 @@
     rows = P(("x", "y", "core", "z"), None)
     in_specs = (rows, rows, rows, P(("x", "y", "core"), None), P(), P())
 
-
     return jax.shard_map(body, mesh=grid, in_specs=in_specs, out_specs=rows, check_vma=False)

time: 88.6 us -> 101 us (1.14)
  starting transfers between devices: 44.9 us -> 59.6 us
  waiting for transfers between devices: 12.2 us -> 10.7 us
    ppermute x8 -> x16, starting transfers between devices: 11 us -> 22.2 us  [the longest x8 13 us: body(): near = [lax.ppermute(part, ('core', 'z'), RING) for part in near]]
    ppermute x7 -> x13, starting transfers between devices: 11.5 us -> 14.9 us  [swap(): return lax.ppermute(value, 'core', SWAP)]
    ppermute x8 -> x16, waiting for transfers between devices: 3.14 us -> 0.61 us  [the longest x8 0.59 us: body(): far = [lax.ppermute(part, ('core', 'z'), RING) for part in far]]
    pallas_call x5 -> x6, Pallas kernels: 15 us -> 14.2 us  [the longest x2 6.88 us: body(): call(functools.partial(step_kernel, order, out is None), sds(whole, BF),...]
    unnamed x8 -> x10, local copies, waits for them, and re-layouts: 4.02 us -> 4.08 us
  transfers between devices with their start and end apart: 23 -> 37, of which waited for: 5 -> 6; matrix products, arithmetic and copies ran while one was open for 1% -> 0% of each run, Pallas kernels for 20% -> 19%
where the time goes in v1:
time: 101 us; the launch traced here: 100 us
  starting transfers between devices  59.6 us (59%)
  Pallas kernels  24.9 us (25%)
  waiting for transfers between devices  10.7 us (11%)
  local copies, waits for them, and re-layouts  4.25 us (4%)
    ppermute x13, starting transfers between devices, swap(): return lax.ppermute(value, 'core', SWAP)  14.9 us
    ppermute x8, starting transfers between devices, body(): near = [lax.ppermute(part, ('core', 'z'), RING) for part in near]  13 us
    ppermute x8, starting transfers between devices, body(): far = [lax.ppermute(part, ('core', 'z'), RING) for part in far]  9.17 us
    all_to_all x1, starting transfers between devices, body(): lax.all_to_all(states, 'z', split_axis=0, concat_axis=0, tiled=True)  9.02 us
    pallas_call x2, Pallas kernels, body(): call(functools.partial(step_kernel, order, out is None), sds(whole, BF),...  6.88 us
    all_to_all x1, waiting for transfers between devices, body(): lax.all_to_all(states, 'z', split_axis=0, concat_axis=0, tiled=True)  6.83 us
    pallas_call x1, Pallas kernels, body(): call(local_kernel, (sds(whole, F32), sds((HEADS, tokens, LEVELS * DH), BF...  6.68 us
    ppermute x2, starting transfers between devices, to_others(): a2 = lax.ppermute(value, axis, shift(4, 2))  5.07 us
  transfers between devices with their start and end apart: 37, of which 6 were waited for; matrix products, arithmetic and copies ran while one was open for 0% of the time, Pallas kernels for 19%

profile of v1, /device:TPU:1, one launch (start us, length us, event | category | flops | bytes accessed | tf_op | source)
XLA Modules:
  0.0 100.0 jit_solution(6079018594368242735)
XLA Ops:
  0.0 3.0 %shard_map.64 = bf16[16,128,128]{2,1,0:T(8,128)(2,1)} custom-call(bf16[256,2048]{1,0:T(8,128)(2,1)} %k_hbm.3, bf16[256,2048]{1,0:T(8,128)(2,1)} %v_hbm.3), custom_call_target="tpu_custom_call" | custom-call | flops 134217728 | bytes 3145728 | tf_op jit(solution)/shard_map/pallas_call | solution.py:296
  3.1 9.0 %all-to-all-start = ((bf16[16,128,128]{2,1,0:T(8,128)(2,1)}), bf16[16,128,128]{2,1,0:T(8,128)(2,1)S(1)}, u32[]{:S(2)}, u32[]{:S(2)}) async-start(bf16[16,128,128]{2,1,0:T(8,128)(2,1)} %shard_map.64), calls=%async_computation | async-start | bytes 1048576 | tf_op jit(solution)/shard_map/all_to_all | solution.py:300
  12.4 6.7 %shard_map.65 = (f32[256,2048]{1,0:T(8,128)S(1)}, bf16[16,256,768]{2,1,0:T(8,128)(2,1)S(1)}) custom-call(bf16[256,2048]{1,0:T(8,128)(2,1)} %q_hbm.1, bf16[256,2048]{1,0:T(8,128)(2,1)} %k_hbm.3, bf16[256,2048]{1,0:T(8,128)(2,1)} %v_hbm.3, s32[6,256]{1,0:T(8,128)S(1)} %dynamic-slice_bitcast_fusion.codes_ref, bf16[128,128]{1,0:T(8,128)(2,1)S(1)} %pad.4.table_ref), custom_call_target="tpu_custom_call" | custom-call | flops 536870912 | bytes 12582912 | tf_op jit(solution)/shard_map/pallas_call | solution.py:305
  19.1 2.7 %copy-done.1 = bf16[16,256,768]{2,1,0:T(8,128)(2,1)} copy-done((bf16[16,256,768]{2,1,0:T(8,128)(2,1)}, bf16[16,256,768]{2,1,0:T(8,128)(2,1)S(1)}, u32[]{:S(2)}) %copy-start.1) | copy-done | bytes 6291480
  21.8 1.4 %copy-done.2 = f32[256,2048]{1,0:T(8,128)} copy-done((f32[256,2048]{1,0:T(8,128)}, f32[256,2048]{1,0:T(8,128)S(1)}, u32[]{:S(2)}) %copy-start.2) | copy-done | bytes 2097176
  23.2 6.8 %all-to-all-done = bf16[16,128,128]{2,1,0:T(8,128)(2,1)S(1)} async-done(((bf16[16,128,128]{2,1,0:T(8,128)(2,1)}), bf16[16,128,128]{2,1,0:T(8,128)(2,1)S(1)}, u32[]{:S(2)}, u32[]{:S(2)}) %all-to-all-start) | async-done | bytes 524320 | tf_op jit(solution)/shard_map/all_to_all | solution.py:300
  30.9 3.5 %all-to-all-start.1 = ((bf16[16,128,128]{2,1,0:T(8,128)(2,1)}), bf16[16,128,128]{2,1,0:T(8,128)(2,1)S(1)}, u32[]{:S(2)}, u32[]{:S(2)}) async-start(bf16[16,128,128]{2,1,0:T(8,128)(2,1)} %bitcast.6), calls=%async_computation.1 | async-start | bytes 1048576 | tf_op jit(solution)/shard_map/all_to_all | solution.py:322
  36.1 1.4 %collective-permute-start.1 = (bf16[256,128]{1,0:T(8,128)(2,1)S(1)}, bf16[256,128]{1,0:T(8,128)(2,1)S(1)}, u32[]{:S(2)}, u32[]{:S(2)}) collective-permute-start(bf16[256,128]{1,0:T(8,128)(2,1)S(1)} %get-tuple-element.25), channel_id=1, source_target_pairs={{0,16},{16,32},{32,48},{48,0},{1,17},{17,33},{33,49},{49,1},{2,18}... | collective-permute-start | bytes 196616 | tf_op jit(solution)/shard_map/ppermute | solution.py:277
  37.5 2.6 %collective-permute-start.2 = (bf16[256,128]{1,0:T(8,128)(2,1)S(1)}, bf16[256,128]{1,0:T(8,128)(2,1)S(1)}, u32[]{:S(2)}, u32[]{:S(2)}) collective-permute-start(bf16[256,128]{1,0:T(8,128)(2,1)S(1)} %get-tuple-element.25), channel_id=1, source_target_pairs={{0,32},{16,48},{32,0},{48,16},{1,33},{17,49},{33,1},{49,17},{2,34}... | collective-permute-start | bytes 196616 | tf_op jit(solution)/shard_map/ppermute | solution.py:276
  41.2 2.1 %collective-permute-done.2.a2_ref = bf16[256,128]{1,0:T(8,128)(2,1)S(1)} collective-permute-done((bf16[256,128]{1,0:T(8,128)(2,1)S(1)}, bf16[256,128]{1,0:T(8,128)(2,1)S(1)}, u32[]{:S(2)}, u32[]{:S(2)}) %collective-permute-start.2) | collective-permute-done | bytes 65568 | tf_op jit(solution)/shard_map/ppermute | solution.py:276
  44.1 1.3 %collective-permute-start.4 = (bf16[256,128]{1,0:T(8,128)(2,1)S(1)}, bf16[256,128]{1,0:T(8,128)(2,1)S(1)}, u32[]{:S(2)}, u32[]{:S(2)}) collective-permute-start(bf16[256,128]{1,0:T(8,128)(2,1)S(1)} %get-tuple-element.27), channel_id=1, source_target_pairs={{0,64},{64,128},{128,192},{192,0},{1,65},{65,129},{129,193},{193,1... | collective-permute-start | bytes 196616 | tf_op jit(solution)/shard_map/ppermute | solution.py:277
  45.4 2.4 %collective-permute-start.5 = (bf16[256,128]{1,0:T(8,128)(2,1)S(1)}, bf16[256,128]{1,0:T(8,128)(2,1)S(1)}, u32[]{:S(2)}, u32[]{:S(2)}) collective-permute-start(bf16[256,128]{1,0:T(8,128)(2,1)S(1)} %get-tuple-element.27), channel_id=1, source_target_pairs={{0,128},{64,192},{128,0},{192,64},{1,129},{65,193},{129,1},{193,65... | collective-permute-start | bytes 196616 | tf_op jit(solution)/shard_map/ppermute | solution.py:276
  47.9 1.2 %collective-permute-start.6 = (bf16[256,128]{1,0:T(8,128)(2,1)S(1)}, bf16[256,128]{1,0:T(8,128)(2,1)S(1)}, u32[]{:S(2)}, u32[]{:S(2)}) collective-permute-start(bf16[256,128]{1,0:T(8,128)(2,1)S(1)} %get-tuple-element.27), channel_id=1, source_target_pairs={{0,192},{64,0},{128,64},{192,128},{1,193},{65,1},{129,65},{193,129... | collective-permute-start | bytes 196616 | tf_op jit(solution)/shard_map/ppermute | solution.py:278
  49.0 2.9 %collective-permute-start.7 = (bf16[384,128]{1,0:T(8,128)(2,1)S(1)}, bf16[384,128]{1,0:T(8,128)(2,1)S(1)}, u32[]{:S(2)}, u32[]{:S(2)}) collective-permute-start(bf16[384,128]{1,0:T(8,128)(2,1)S(1)} %get-tuple-element.26.refs_4_), channel_id=1, source_target_pairs={{0,1},{1,2},{2,3},{3,4},{4,5},{5,6},{6,7},{7,0},{8,15},{9,8},{10,9... | collective-permute-start | bytes 294920 | tf_op jit(solution)/shard_map/ppermute | solution.py:341
  51.9 1.2 %collective-permute-start.9 = (bf16[384,128]{1,0:T(8,128)(2,1)S(1)}, bf16[384,128]{1,0:T(8,128)(2,1)S(1)}, u32[]{:S(2)}, u32[]{:S(2)}) collective-permute-start(bf16[384,128]{1,0:T(8,128)(2,1)S(1)} %get-tuple-element.29.refs_6_), channel_id=1, source_target_pairs={{0,1},{1,2},{2,3},{3,4},{4,5},{5,6},{6,7},{7,0},{8,15},{9,8},{10,9... | collective-permute-start | bytes 294920 | tf_op jit(solution)/shard_map/ppermute | solution.py:341
  53.7 1.3 %collective-permute-start.8 = (bf16[256,128]{1,0:T(8,128)(2,1)S(1)}, bf16[256,128]{1,0:T(8,128)(2,1)S(1)}, u32[]{:S(2)}, u32[]{:S(2)}) collective-permute-start(bf16[256,128]{1,0:T(8,128)(2,1)S(1)} %get-tuple-element.28.refs_5_), channel_id=1, source_target_pairs={{0,1},{1,2},{2,3},{3,4},{4,5},{5,6},{6,7},{7,0},{8,15},{9,8},{10,9... | collective-permute-start | bytes 196616 | tf_op jit(solution)/shard_map/ppermute | solution.py:342
  54.9 2.5 %collective-permute-start.11 = (bf16[384,128]{1,0:T(8,128)(2,1)S(1)}, bf16[384,128]{1,0:T(8,128)(2,1)S(1)}, u32[]{:S(2)}, u32[]{:S(2)}) collective-permute-start(bf16[384,128]{1,0:T(8,128)(2,1)S(1)} %collective-permute-done.7.refs_5_), channel_id=1, source_target_pairs={{0,8},{8,0},{1,9},{9,1},{2,10},{10,2},{3,11},{11,3},{4,12},{12,4},... | collective-permute-start | bytes 294920 | tf_op jit(solution)/shard_map/ppermute | solution.py:283
  57.5 1.9 %collective-permute-start.13 = (bf16[384,128]{1,0:T(8,128)(2,1)S(1)}, bf16[384,128]{1,0:T(8,128)(2,1)S(1)}, u32[]{:S(2)}, u32[]{:S(2)}) collective-permute-start(bf16[384,128]{1,0:T(8,128)(2,1)S(1)} %collective-permute-done.9.refs_7_), channel_id=1, source_target_pairs={{0,8},{8,0},{1,9},{9,1},{2,10},{10,2},{3,11},{11,3},{4,12},{12,4},... | collective-permute-start | bytes 294920 | tf_op jit(solution)/shard_map/ppermute | solution.py:283
  61.2 1.2 %collective-permute-start.16 = (bf16[256,128]{1,0:T(8,128)(2,1)S(1)}, bf16[256,128]{1,0:T(8,128)(2,1)S(1)}, u32[]{:S(2)}, u32[]{:S(2)}) collective-permute-start(bf16[256,128]{1,0:T(8,128)(2,1)S(1)} %collective-permute-done.8.refs_6_), channel_id=1, source_target_pairs={{0,1},{1,2},{2,3},{3,4},{4,5},{5,6},{6,7},{7,0},{8,15},{9,8},{10,9... | collective-permute-start | bytes 196616 | tf_op jit(solution)/shard_map/ppermute | solution.py:342
  62.5 2.0 %collective-permute-start.15 = (bf16[384,128]{1,0:T(8,128)(2,1)S(1)}, bf16[384,128]{1,0:T(8,128)(2,1)S(1)}, u32[]{:S(2)}, u32[]{:S(2)}) collective-permute-start(bf16[384,128]{1,0:T(8,128)(2,1)S(1)} %collective-permute-done.7.refs_5_), channel_id=1, source_target_pairs={{0,1},{1,2},{2,3},{3,4},{4,5},{5,6},{6,7},{7,0},{8,15},{9,8},{10,9... | collective-permute-start | bytes 294920 | tf_op jit(solution)/shard_map/ppermute | solution.py:341
  64.9 2.1 %collective-permute-start.18 = (bf16[256,128]{1,0:T(8,128)(2,1)S(1)}, bf16[256,128]{1,0:T(8,128)(2,1)S(1)}, u32[]{:S(2)}, u32[]{:S(2)}) collective-permute-start(bf16[256,128]{1,0:T(8,128)(2,1)S(1)} %collective-permute-done.10.refs_8_), channel_id=1, source_target_pairs={{0,1},{1,2},{2,3},{3,4},{4,5},{5,6},{6,7},{7,0},{8,15},{9,8},{10,9... | collective-permute-start | bytes 196616 | tf_op jit(solution)/shard_map/ppermute | solution.py:342
  68.7 3.8 %collective-permute-start.22 = (bf16[256,128]{1,0:T(8,128)(2,1)S(1)}, bf16[256,128]{1,0:T(8,128)(2,1)S(1)}, u32[]{:S(2)}, u32[]{:S(2)}) collective-permute-start(bf16[256,128]{1,0:T(8,128)(2,1)S(1)} %collective-permute-done.18.refs_3_), channel_id=1, source_target_pairs={{0,8},{8,0},{1,9},{9,1},{2,10},{10,2},{3,11},{11,3},{4,12},{12,4},... | collective-permute-start | bytes 196616 | tf_op jit(solution)/shard_map/ppermute | solution.py:283
  73.7 1.8 %collective-permute-start.26 = (bf16[256,128]{1,0:T(8,128)(2,1)S(1)}, bf16[256,128]{1,0:T(8,128)(2,1)S(1)}, u32[]{:S(2)}, u32[]{:S(2)}) collective-permute-start(bf16[256,128]{1,0:T(8,128)(2,1)S(1)} %collective-permute-done.18.refs_3_), channel_id=1, source_target_pairs={{0,1},{1,2},{2,3},{3,4},{4,5},{5,6},{6,7},{7,0},{8,15},{9,8},{10,9... | collective-permute-start | bytes 196616 | tf_op jit(solution)/shard_map/ppermute | solution.py:342
  75.6 2.9 %collective-permute-start.25 = (bf16[384,128]{1,0:T(8,128)(2,1)S(1)}, bf16[384,128]{1,0:T(8,128)(2,1)S(1)}, u32[]{:S(2)}, u32[]{:S(2)}) collective-permute-start(bf16[384,128]{1,0:T(8,128)(2,1)S(1)} %collective-permute-done.17.refs_2_), channel_id=1, source_target_pairs={{0,1},{1,2},{2,3},{3,4},{4,5},{5,6},{6,7},{7,0},{8,15},{9,8},{10,9... | collective-permute-start | bytes 294920 | tf_op jit(solution)/shard_map/ppermute | solution.py:341
  78.5 1.1 %collective-permute-start.28 = (bf16[256,128]{1,0:T(8,128)(2,1)S(1)}, bf16[256,128]{1,0:T(8,128)(2,1)S(1)}, u32[]{:S(2)}, u32[]{:S(2)}) collective-permute-start(bf16[256,128]{1,0:T(8,128)(2,1)S(1)} %collective-permute-done.24.refs_9_), channel_id=1, source_target_pairs={{0,8},{8,0},{1,9},{9,1},{2,10},{10,2},{3,11},{11,3},{4,12},{12,4},... | collective-permute-start | bytes 196616 | tf_op jit(solution)/shard_map/ppermute | solution.py:283
  79.7 1.2 %collective-permute-start.32 = (bf16[256,128]{1,0:T(8,128)(2,1)S(1)}, bf16[256,128]{1,0:T(8,128)(2,1)S(1)}, u32[]{:S(2)}, u32[]{:S(2)}) collective-permute-start(bf16[256,128]{1,0:T(8,128)(2,1)S(1)} %collective-permute-done.24.refs_9_), channel_id=1, source_target_pairs={{0,1},{1,2},{2,3},{3,4},{4,5},{5,6},{6,7},{7,0},{8,15},{9,8},{10,9... | collective-permute-start | bytes 196616 | tf_op jit(solution)/shard_map/ppermute | solution.py:342
  81.0 1.2 %collective-permute-start.27 = (bf16[384,128]{1,0:T(8,128)(2,1)S(1)}, bf16[384,128]{1,0:T(8,128)(2,1)S(1)}, u32[]{:S(2)}, u32[]{:S(2)}) collective-permute-start(bf16[384,128]{1,0:T(8,128)(2,1)S(1)} %collective-permute-done.23.refs_8_), channel_id=1, source_target_pairs={{0,8},{8,0},{1,9},{9,1},{2,10},{10,2},{3,11},{11,3},{4,12},{12,4},... | collective-permute-start | bytes 294920 | tf_op jit(solution)/shard_map/ppermute | solution.py:283
  84.3 2.4 %collective-permute-start.33 = (bf16[384,128]{1,0:T(8,128)(2,1)S(1)}, bf16[384,128]{1,0:T(8,128)(2,1)S(1)}, u32[]{:S(2)}, u32[]{:S(2)}) collective-permute-start(bf16[384,128]{1,0:T(8,128)(2,1)S(1)} %collective-permute-done.25.refs_10_), channel_id=1, source_target_pairs={{0,1},{1,2},{2,3},{3,4},{4,5},{5,6},{6,7},{7,0},{8,15},{9,8},{10,9... | collective-permute-start | bytes 294920 | tf_op jit(solution)/shard_map/ppermute | solution.py:341
  86.8 3.6 %shard_map.73 = (bf16[10,256,640]{2,1,0:T(8,128)(2,1)S(1)}, f32[10,256,128]{2,1,0:T(8,128)S(1)}) custom-call(s32[4]{0:T(128)S(1)} %pad_add_fusion.pos_ref, bf16[16,256,768]{2,1,0:T(8,128)(2,1)} %copy-done.1, f32[256,2048]{1,0:T(8,128)} %copy-done.2, bf16[16,128,128]{2,1,0:T(8,128)(2,1)S(1)} %all-to-all-done.1.refs_2_.refs_3_.p_hbm), custom_call_target="tpu_custom_call" | custom-call | flops 83886080 | bytes 5242880 | tf_op jit(solution)/shard_map/pallas_call | solution.py:364
  90.4 3.0 %shard_map.71.refs_0_ = bf16[256,2048]{1,0:T(8,128)(2,1)} custom-call(s32[4]{0:T(128)S(1)} %pad_add_fusion.pos_ref, bf16[16,256,768]{2,1,0:T(8,128)(2,1)} %copy-done.1, f32[256,2048]{1,0:T(8,128)} %copy-done.2, bf16[16,128,128]{2,1,0:T(8,128)(2,1)S(1)} %all-to-all-done.1.refs_2_.refs_3_.p_hbm, f32[16,128]{1,0:T(8,128)S(1)} %copy-done.3, ...), custom_call_target="tpu_custom_call" | custom-call | flops 100663296 | bytes 1048576 | tf_op jit(solution)/shard_map/pallas_call | solution.py:350
  93.5 3.9 %shard_map.72.prev_hbm = bf16[256,2048]{1,0:T(8,128)(2,1)} custom-call(s32[4]{0:T(128)S(1)} %pad_add_fusion.pos_ref, bf16[256,2048]{1,0:T(8,128)(2,1)} %shard_map.71.refs_0_, bf16[16,256,768]{2,1,0:T(8,128)(2,1)} %copy-done.1, f32[256,2048]{1,0:T(8,128)} %copy-done.2, ...), custom_call_target="tpu_custom_call", output_to_operand_aliasing={{}: (1, {})} | custom-call | flops 201326592 | bytes 2097152 | tf_op jit(solution)/shard_map/pallas_call | solution.py:350
  97.4 2.4 %shard_map.74 = bf16[256,2048]{1,0:T(8,128)(2,1)} custom-call(s32[4]{0:T(128)S(1)} %pad_add_fusion.pos_ref, bf16[256,2048]{1,0:T(8,128)(2,1)} %shard_map.72.prev_hbm, bf16[10,256,640]{2,1,0:T(8,128)(2,1)S(1)} %get-tuple-element.31.qw_ref, f32[10,256,128]{2,1,0:T(8,128)S(1)} %get-tuple-element.32.acc_ref, ...), custom_call_target="tpu_custom_call", output_to_operand_aliasing={{}: (1, {})} | custom-call | flops 419430400 | bytes 5242880 | tf_op jit(solution)/shard_map/pallas_call | solution.py:370
  (70 shorter events, 13.1 us)
Async XLA Ops:
  3.1 27.0 %all-to-all-start = ((bf16[16,128,128]{2,1,0:T(8,128)(2,1)}), bf16[16,128,128]{2,1,0:T(8,128)(2,1)S(1)}, u32[]{:S(2)}, u32[]{:S(2)}) async-start(bf16[16,128,128]{2,1,0:T(8,128)(2,1)} %shard_map.64), calls=%async_computation | async-start | bytes 1048576 | tf_op jit(solution)/shard_map/all_to_all | solution.py:300
  30.9 55.9 %all-to-all-start.1 = ((bf16[16,128,128]{2,1,0:T(8,128)(2,1)}), bf16[16,128,128]{2,1,0:T(8,128)(2,1)S(1)}, u32[]{:S(2)}, u32[]{:S(2)}) async-start(bf16[16,128,128]{2,1,0:T(8,128)(2,1)} %bitcast.6), calls=%async_computation.1 | async-start | bytes 1048576 | tf_op jit(solution)/shard_map/all_to_all | solution.py:322
  36.1 5.1 %collective-permute-start.1 = (bf16[256,128]{1,0:T(8,128)(2,1)S(1)}, bf16[256,128]{1,0:T(8,128)(2,1)S(1)}, u32[]{:S(2)}, u32[]{:S(2)}) collective-permute-start(bf16[256,128]{1,0:T(8,128)(2,1)S(1)} %get-tuple-element.25), channel_id=1, source_target_pairs={{0,16},{16,32},{32,48},{48,0},{1,17},{17,33},{33,49},{49,1},{2,18}... | collective-permute-start | bytes 196616 | tf_op jit(solution)/shard_map/ppermute | solution.py:277
  37.5 5.8 %collective-permute-start.2 = (bf16[256,128]{1,0:T(8,128)(2,1)S(1)}, bf16[256,128]{1,0:T(8,128)(2,1)S(1)}, u32[]{:S(2)}, u32[]{:S(2)}) collective-permute-start(bf16[256,128]{1,0:T(8,128)(2,1)S(1)} %get-tuple-element.25), channel_id=1, source_target_pairs={{0,32},{16,48},{32,0},{48,16},{1,33},{17,49},{33,1},{49,17},{2,34}... | collective-permute-start | bytes 196616 | tf_op jit(solution)/shard_map/ppermute | solution.py:276
  44.1 9.0 %collective-permute-start.4 = (bf16[256,128]{1,0:T(8,128)(2,1)S(1)}, bf16[256,128]{1,0:T(8,128)(2,1)S(1)}, u32[]{:S(2)}, u32[]{:S(2)}) collective-permute-start(bf16[256,128]{1,0:T(8,128)(2,1)S(1)} %get-tuple-element.27), channel_id=1, source_target_pairs={{0,64},{64,128},{128,192},{192,0},{1,65},{65,129},{129,193},{193,1... | collective-permute-start | bytes 196616 | tf_op jit(solution)/shard_map/ppermute | solution.py:277
  45.4 7.7 %collective-permute-start.5 = (bf16[256,128]{1,0:T(8,128)(2,1)S(1)}, bf16[256,128]{1,0:T(8,128)(2,1)S(1)}, u32[]{:S(2)}, u32[]{:S(2)}) collective-permute-start(bf16[256,128]{1,0:T(8,128)(2,1)S(1)} %get-tuple-element.27), channel_id=1, source_target_pairs={{0,128},{64,192},{128,0},{192,64},{1,129},{65,193},{129,1},{193,65... | collective-permute-start | bytes 196616 | tf_op jit(solution)/shard_map/ppermute | solution.py:276
  47.9 5.2 %collective-permute-start.6 = (bf16[256,128]{1,0:T(8,128)(2,1)S(1)}, bf16[256,128]{1,0:T(8,128)(2,1)S(1)}, u32[]{:S(2)}, u32[]{:S(2)}) collective-permute-start(bf16[256,128]{1,0:T(8,128)(2,1)S(1)} %get-tuple-element.27), channel_id=1, source_target_pairs={{0,192},{64,0},{128,64},{192,128},{1,193},{65,1},{129,65},{193,129... | collective-permute-start | bytes 196616 | tf_op jit(solution)/shard_map/ppermute | solution.py:278
  49.0 5.9 %collective-permute-start.7 = (bf16[384,128]{1,0:T(8,128)(2,1)S(1)}, bf16[384,128]{1,0:T(8,128)(2,1)S(1)}, u32[]{:S(2)}, u32[]{:S(2)}) collective-permute-start(bf16[384,128]{1,0:T(8,128)(2,1)S(1)} %get-tuple-element.26.refs_4_), channel_id=1, source_target_pairs={{0,1},{1,2},{2,3},{3,4},{4,5},{5,6},{6,7},{7,0},{8,15},{9,8},{10,9... | collective-permute-start | bytes 294920 | tf_op jit(solution)/shard_map/ppermute | solution.py:341
  51.9 5.6 %collective-permute-start.9 = (bf16[384,128]{1,0:T(8,128)(2,1)S(1)}, bf16[384,128]{1,0:T(8,128)(2,1)S(1)}, u32[]{:S(2)}, u32[]{:S(2)}) collective-permute-start(bf16[384,128]{1,0:T(8,128)(2,1)S(1)} %get-tuple-element.29.refs_6_), channel_id=1, source_target_pairs={{0,1},{1,2},{2,3},{3,4},{4,5},{5,6},{6,7},{7,0},{8,15},{9,8},{10,9... | collective-permute-start | bytes 294920 | tf_op jit(solution)/shard_map/ppermute | solution.py:341
  53.7 6.5 %collective-permute-start.8 = (bf16[256,128]{1,0:T(8,128)(2,1)S(1)}, bf16[256,128]{1,0:T(8,128)(2,1)S(1)}, u32[]{:S(2)}, u32[]{:S(2)}) collective-permute-start(bf16[256,128]{1,0:T(8,128)(2,1)S(1)} %get-tuple-element.28.refs_5_), channel_id=1, source_target_pairs={{0,1},{1,2},{2,3},{3,4},{4,5},{5,6},{6,7},{7,0},{8,15},{9,8},{10,9... | collective-permute-start | bytes 196616 | tf_op jit(solution)/shard_map/ppermute | solution.py:342
  54.9 9.6 %collective-permute-start.11 = (bf16[384,128]{1,0:T(8,128)(2,1)S(1)}, bf16[384,128]{1,0:T(8,128)(2,1)S(1)}, u32[]{:S(2)}, u32[]{:S(2)}) collective-permute-start(bf16[384,128]{1,0:T(8,128)(2,1)S(1)} %collective-permute-done.7.refs_5_), channel_id=1, source_target_pairs={{0,8},{8,0},{1,9},{9,1},{2,10},{10,2},{3,11},{11,3},{4,12},{12,4},... | collective-permute-start | bytes 294920 | tf_op jit(solution)/shard_map/ppermute | solution.py:283
  57.5 9.6 %collective-permute-start.13 = (bf16[384,128]{1,0:T(8,128)(2,1)S(1)}, bf16[384,128]{1,0:T(8,128)(2,1)S(1)}, u32[]{:S(2)}, u32[]{:S(2)}) collective-permute-start(bf16[384,128]{1,0:T(8,128)(2,1)S(1)} %collective-permute-done.9.refs_7_), channel_id=1, source_target_pairs={{0,8},{8,0},{1,9},{9,1},{2,10},{10,2},{3,11},{11,3},{4,12},{12,4},... | collective-permute-start | bytes 294920 | tf_op jit(solution)/shard_map/ppermute | solution.py:283
  60.2 4.8 %collective-permute-start.12 = (bf16[256,128]{1,0:T(8,128)(2,1)S(1)}, bf16[256,128]{1,0:T(8,128)(2,1)S(1)}, u32[]{:S(2)}, u32[]{:S(2)}) collective-permute-start(bf16[256,128]{1,0:T(8,128)(2,1)S(1)} %collective-permute-done.8.refs_6_), channel_id=1, source_target_pairs={{0,8},{8,0},{1,9},{9,1},{2,10},{10,2},{3,11},{11,3},{4,12},{12,4},... | collective-permute-start | bytes 196616 | tf_op jit(solution)/shard_map/ppermute | solution.py:283
  61.2 7.0 %collective-permute-start.16 = (bf16[256,128]{1,0:T(8,128)(2,1)S(1)}, bf16[256,128]{1,0:T(8,128)(2,1)S(1)}, u32[]{:S(2)}, u32[]{:S(2)}) collective-permute-start(bf16[256,128]{1,0:T(8,128)(2,1)S(1)} %collective-permute-done.8.refs_6_), channel_id=1, source_target_pairs={{0,1},{1,2},{2,3},{3,4},{4,5},{5,6},{6,7},{7,0},{8,15},{9,8},{10,9... | collective-permute-start | bytes 196616 | tf_op jit(solution)/shard_map/ppermute | solution.py:342
  62.5 10.7 %collective-permute-start.15 = (bf16[384,128]{1,0:T(8,128)(2,1)S(1)}, bf16[384,128]{1,0:T(8,128)(2,1)S(1)}, u32[]{:S(2)}, u32[]{:S(2)}) collective-permute-start(bf16[384,128]{1,0:T(8,128)(2,1)S(1)} %collective-permute-done.7.refs_5_), channel_id=1, source_target_pairs={{0,1},{1,2},{2,3},{3,4},{4,5},{5,6},{6,7},{7,0},{8,15},{9,8},{10,9... | collective-permute-start | bytes 294920 | tf_op jit(solution)/shard_map/ppermute | solution.py:341
  64.5 8.9 %collective-permute-start.17 = (bf16[384,128]{1,0:T(8,128)(2,1)S(1)}, bf16[384,128]{1,0:T(8,128)(2,1)S(1)}, u32[]{:S(2)}, u32[]{:S(2)}) collective-permute-start(bf16[384,128]{1,0:T(8,128)(2,1)S(1)} %collective-permute-done.9.refs_7_), channel_id=1, source_target_pairs={{0,1},{1,2},{2,3},{3,4},{4,5},{5,6},{6,7},{7,0},{8,15},{9,8},{10,9... | collective-permute-start | bytes 294920 | tf_op jit(solution)/shard_map/ppermute | solution.py:341
  67.0 5.4 %collective-permute-start.14 = (bf16[256,128]{1,0:T(8,128)(2,1)S(1)}, bf16[256,128]{1,0:T(8,128)(2,1)S(1)}, u32[]{:S(2)}, u32[]{:S(2)}) collective-permute-start(bf16[256,128]{1,0:T(8,128)(2,1)S(1)} %collective-permute-done.10.refs_8_), channel_id=1, source_target_pairs={{0,8},{8,0},{1,9},{9,1},{2,10},{10,2},{3,11},{11,3},{4,12},{12,4},... | collective-permute-start | bytes 196616 | tf_op jit(solution)/shard_map/ppermute | solution.py:283
  68.2 5.5 %collective-permute-start.20 = (bf16[256,128]{1,0:T(8,128)(2,1)S(1)}, bf16[256,128]{1,0:T(8,128)(2,1)S(1)}, u32[]{:S(2)}, u32[]{:S(2)}) collective-permute-start(bf16[256,128]{1,0:T(8,128)(2,1)S(1)} %collective-permute-done.16.refs_1_), channel_id=1, source_target_pairs={{0,8},{8,0},{1,9},{9,1},{2,10},{10,2},{3,11},{11,3},{4,12},{12,4},... | collective-permute-start | bytes 196616 | tf_op jit(solution)/shard_map/ppermute | solution.py:283
  68.7 6.8 %collective-permute-start.22 = (bf16[256,128]{1,0:T(8,128)(2,1)S(1)}, bf16[256,128]{1,0:T(8,128)(2,1)S(1)}, u32[]{:S(2)}, u32[]{:S(2)}) collective-permute-start(bf16[256,128]{1,0:T(8,128)(2,1)S(1)} %collective-permute-done.18.refs_3_), channel_id=1, source_target_pairs={{0,8},{8,0},{1,9},{9,1},{2,10},{10,2},{3,11},{11,3},{4,12},{12,4},... | collective-permute-start | bytes 196616 | tf_op jit(solution)/shard_map/ppermute | solution.py:283
  73.1 6.5 %collective-permute-start.19 = (bf16[384,128]{1,0:T(8,128)(2,1)S(1)}, bf16[384,128]{1,0:T(8,128)(2,1)S(1)}, u32[]{:S(2)}, u32[]{:S(2)}) collective-permute-start(bf16[384,128]{1,0:T(8,128)(2,1)S(1)} %collective-permute-done.15.refs_0_), channel_id=1, source_target_pairs={{0,8},{8,0},{1,9},{9,1},{2,10},{10,2},{3,11},{11,3},{4,12},{12,4},... | collective-permute-start | bytes 294920 | tf_op jit(solution)/shard_map/ppermute | solution.py:283
  73.5 6.3 %collective-permute-start.21 = (bf16[384,128]{1,0:T(8,128)(2,1)S(1)}, bf16[384,128]{1,0:T(8,128)(2,1)S(1)}, u32[]{:S(2)}, u32[]{:S(2)}) collective-permute-start(bf16[384,128]{1,0:T(8,128)(2,1)S(1)} %collective-permute-done.17.refs_2_), channel_id=1, source_target_pairs={{0,8},{8,0},{1,9},{9,1},{2,10},{10,2},{3,11},{11,3},{4,12},{12,4},... | collective-permute-start | bytes 294920 | tf_op jit(solution)/shard_map/ppermute | solution.py:283
  73.7 4.9 %collective-permute-start.26 = (bf16[256,128]{1,0:T(8,128)(2,1)S(1)}, bf16[256,128]{1,0:T(8,128)(2,1)S(1)}, u32[]{:S(2)}, u32[]{:S(2)}) collective-permute-start(bf16[256,128]{1,0:T(8,128)(2,1)S(1)} %collective-permute-done.18.refs_3_), channel_id=1, source_target_pairs={{0,1},{1,2},{2,3},{3,4},{4,5},{5,6},{6,7},{7,0},{8,15},{9,8},{10,9... | collective-permute-start | bytes 196616 | tf_op jit(solution)/shard_map/ppermute | solution.py:342
  75.5 5.5 %collective-permute-start.23 = (bf16[384,128]{1,0:T(8,128)(2,1)S(1)}, bf16[384,128]{1,0:T(8,128)(2,1)S(1)}, u32[]{:S(2)}, u32[]{:S(2)}) collective-permute-start(bf16[384,128]{1,0:T(8,128)(2,1)S(1)} %collective-permute-done.15.refs_0_), channel_id=1, source_target_pairs={{0,1},{1,2},{2,3},{3,4},{4,5},{5,6},{6,7},{7,0},{8,15},{9,8},{10,9... | collective-permute-start | bytes 294920 | tf_op jit(solution)/shard_map/ppermute | solution.py:341
  75.6 6.6 %collective-permute-start.25 = (bf16[384,128]{1,0:T(8,128)(2,1)S(1)}, bf16[384,128]{1,0:T(8,128)(2,1)S(1)}, u32[]{:S(2)}, u32[]{:S(2)}) collective-permute-start(bf16[384,128]{1,0:T(8,128)(2,1)S(1)} %collective-permute-done.17.refs_2_), channel_id=1, source_target_pairs={{0,1},{1,2},{2,3},{3,4},{4,5},{5,6},{6,7},{7,0},{8,15},{9,8},{10,9... | collective-permute-start | bytes 294920 | tf_op jit(solution)/shard_map/ppermute | solution.py:341
  78.5 4.7 %collective-permute-start.28 = (bf16[256,128]{1,0:T(8,128)(2,1)S(1)}, bf16[256,128]{1,0:T(8,128)(2,1)S(1)}, u32[]{:S(2)}, u32[]{:S(2)}) collective-permute-start(bf16[256,128]{1,0:T(8,128)(2,1)S(1)} %collective-permute-done.24.refs_9_), channel_id=1, source_target_pairs={{0,8},{8,0},{1,9},{9,1},{2,10},{10,2},{3,11},{11,3},{4,12},{12,4},... | collective-permute-start | bytes 196616 | tf_op jit(solution)/shard_map/ppermute | solution.py:283
  79.7 4.6 %collective-permute-start.30 = (bf16[256,128]{1,0:T(8,128)(2,1)S(1)}, bf16[256,128]{1,0:T(8,128)(2,1)S(1)}, u32[]{:S(2)}, u32[]{:S(2)}) collective-permute-start(bf16[256,128]{1,0:T(8,128)(2,1)S(1)} %collective-permute-done.26.refs_11_), channel_id=1, source_target_pairs={{0,8},{8,0},{1,9},{9,1},{2,10},{10,2},{3,11},{11,3},{4,12},{12,4},... | collective-permute-start | bytes 196616 | tf_op jit(solution)/shard_map/ppermute | solution.py:283
  79.7 7.0 %collective-permute-start.32 = (bf16[256,128]{1,0:T(8,128)(2,1)S(1)}, bf16[256,128]{1,0:T(8,128)(2,1)S(1)}, u32[]{:S(2)}, u32[]{:S(2)}) collective-permute-start(bf16[256,128]{1,0:T(8,128)(2,1)S(1)} %collective-permute-done.24.refs_9_), channel_id=1, source_target_pairs={{0,1},{1,2},{2,3},{3,4},{4,5},{5,6},{6,7},{7,0},{8,15},{9,8},{10,9... | collective-permute-start | bytes 196616 | tf_op jit(solution)/shard_map/ppermute | solution.py:342
  81.0 16.4 %collective-permute-start.27 = (bf16[384,128]{1,0:T(8,128)(2,1)S(1)}, bf16[384,128]{1,0:T(8,128)(2,1)S(1)}, u32[]{:S(2)}, u32[]{:S(2)}) collective-permute-start(bf16[384,128]{1,0:T(8,128)(2,1)S(1)} %collective-permute-done.23.refs_8_), channel_id=1, source_target_pairs={{0,8},{8,0},{1,9},{9,1},{2,10},{10,2},{3,11},{11,3},{4,12},{12,4},... | collective-permute-start | bytes 294920 | tf_op jit(solution)/shard_map/ppermute | solution.py:283
  82.2 15.2 %collective-permute-start.31 = (bf16[384,128]{1,0:T(8,128)(2,1)S(1)}, bf16[384,128]{1,0:T(8,128)(2,1)S(1)}, u32[]{:S(2)}, u32[]{:S(2)}) collective-permute-start(bf16[384,128]{1,0:T(8,128)(2,1)S(1)} %collective-permute-done.23.refs_8_), channel_id=1, source_target_pairs={{0,1},{1,2},{2,3},{3,4},{4,5},{5,6},{6,7},{7,0},{8,15},{9,8},{10,9... | collective-permute-start | bytes 294920 | tf_op jit(solution)/shard_map/ppermute | solution.py:341
  83.2 14.2 %collective-permute-start.29 = (bf16[384,128]{1,0:T(8,128)(2,1)S(1)}, bf16[384,128]{1,0:T(8,128)(2,1)S(1)}, u32[]{:S(2)}, u32[]{:S(2)}) collective-permute-start(bf16[384,128]{1,0:T(8,128)(2,1)S(1)} %collective-permute-done.25.refs_10_), channel_id=1, source_target_pairs={{0,8},{8,0},{1,9},{9,1},{2,10},{10,2},{3,11},{11,3},{4,12},{12,4},... | collective-permute-start | bytes 294920 | tf_op jit(solution)/shard_map/ppermute | solution.py:283
  84.3 13.1 %collective-permute-start.33 = (bf16[384,128]{1,0:T(8,128)(2,1)S(1)}, bf16[384,128]{1,0:T(8,128)(2,1)S(1)}, u32[]{:S(2)}, u32[]{:S(2)}) collective-permute-start(bf16[384,128]{1,0:T(8,128)(2,1)S(1)} %collective-permute-done.25.refs_10_), channel_id=1, source_target_pairs={{0,1},{1,2},{2,3},{3,4},{4,5},{5,6},{6,7},{7,0},{8,15},{9,8},{10,9... | collective-permute-start | bytes 294920 | tf_op jit(solution)/shard_map/ppermute | solution.py:341
  86.7 10.6 %collective-permute-start.34 = (bf16[256,128]{1,0:T(8,128)(2,1)S(1)}, bf16[256,128]{1,0:T(8,128)(2,1)S(1)}, u32[]{:S(2)}, u32[]{:S(2)}) collective-permute-start(bf16[256,128]{1,0:T(8,128)(2,1)S(1)} %collective-permute-done.26.refs_11_), channel_id=1, source_target_pairs={{0,1},{1,2},{2,3},{3,4},{4,5},{5,6},{6,7},{7,0},{8,15},{9,8},{10,9... | collective-permute-start | bytes 196616 | tf_op jit(solution)/shard_map/ppermute | solution.py:342
  (10 other events, 74.7 us)

commit v2 on v1

--- a/solution.py
+++ b/solution.py
@@ -59,9 +59,10 @@
 LOADS = 4
 
 
-def state_kernel(k_hbm, v_hbm, s_ref, k_ref, v_ref, sems):
+def state_kernel(k_hbm, v_hbm, s_hbm, k_ref, v_ref, s_ref, sems, out_sems):
     width = HEADS * DH // LOADS
-    copies = []
+    per = HEADS // LOADS
+    copies, stores = [], []
     for i in range(LOADS):
         cols = pl.ds(i * width, width)
         pair = [
@@ -74,12 +75,18 @@
     for i in range(LOADS):
         for copy in copies[i]:
             copy.wait()
-        for h in range(i * HEADS // LOADS, (i + 1) * HEADS // LOADS):
+        for h in range(i * per, (i + 1) * per):
             s = lax.dot_general(
                 k_ref[:, head_cols(h)], v_ref[:, head_cols(h)], (((0,), (0,)), ((), ())),
                 preferred_element_type=F32,
             )
             s_ref[h] = s.astype(BF)
+        heads = pl.ds(i * per, per)
+        store = pltpu.make_async_copy(s_ref.at[heads], s_hbm.at[heads], out_sems.at[i])
+        store.start()
+        stores.append(store)
+    for store in stores:
+        store.wait()
 
 
 def local_kernel(
@@ -158,28 +165,30 @@
     return (value * jnp.where(flag, 1.0, 0.0)).astype(BF)
 
 
-def put(out_refs, l, value):
+def put(out_ref, l, value):
+    size = out_ref.shape[0] // PER
     for i in range(PER):
-        out_refs[i][l * DH : (l + 1) * DH, :] = value[i * DH : (i + 1) * DH, :]
-
-
-def near_kernel(pos_ref, mine_ref, other_ref, total_ref, a1_ref, a2_ref, a3_ref, *outs):
+        at = i * size + l * DH
+        out_ref[at : at + DH, :] = value[i * DH : (i + 1) * DH, :]
+
+
+def near_kernel(pos_ref, mine_ref, other_ref, total_ref, a1_ref, a2_ref, a3_ref, out_ref, sent_ref):
     y, core = pos_ref[1], pos_ref[2]
     a1, a2, a3 = a1_ref[...].astype(F32), a2_ref[...].astype(F32), a3_ref[...].astype(F32)
-    outs[PER][...] = (total_ref[...] + (a1 + a2 + a3)).astype(BF)
+    sent_ref[...] = (total_ref[...] + (a1 + a2 + a3)).astype(BF)
     two = jnp.where(y == 2, 1.0, 0.0)
     first = jnp.where(core == 0, 1.0, 0.0)
-    put(outs, 0, (mine_ref[...] * first + other_ref[...] * (1.0 - first)).astype(BF))
-    put(outs, 1, on(y % 2 == 1, a1))
-    put(outs, 2, on(y >= 2, a2 + a1 * two + a3 * (1.0 - two)))
-
-
-def far_kernel(pos_ref, a1_ref, a2_ref, a3_ref, *outs):
+    put(out_ref, 0, (mine_ref[...] * first + other_ref[...] * (1.0 - first)).astype(BF))
+    put(out_ref, 1, on(y % 2 == 1, a1))
+    put(out_ref, 2, on(y >= 2, a2 + a1 * two + a3 * (1.0 - two)))
+
+
+def far_kernel(pos_ref, a1_ref, a2_ref, a3_ref, out_ref):
     x = pos_ref[0]
     a1, a2, a3 = a1_ref[...].astype(F32), a2_ref[...].astype(F32), a3_ref[...].astype(F32)
     two = jnp.where(x == 2, 1.0, 0.0)
-    put(outs, 0, on(x % 2 == 1, a1))
-    put(outs, 1, on(x >= 2, a2 + a1 * two + a3 * (1.0 - two)))
+    put(out_ref, 0, on(x % 2 == 1, a1))
+    put(out_ref, 1, on(x >= 2, a2 + a1 * two + a3 * (1.0 - two)))
 
 
 def head_at(pos_ref, order, i):
@@ -188,9 +197,10 @@
 
 
 def finish(i, h, total, scaled, at, states, gain_ref, o_ref, out_hbm, out_sems):
-    for part in states[2 * i : 2 * i + 2]:
-        size = part.shape[0]
-        total = total + jnp.dot(scaled[:, at : at + size], part[...], preferred_element_type=F32)
+    for part in states[i // PER * 2 : i // PER * 2 + 2]:
+        size = part.shape[0] // PER
+        rows = slice(i % PER * size, (i % PER + 1) * size)
+        total = total + jnp.dot(scaled[:, at : at + size], part[rows, :], preferred_element_type=F32)
         at += size
     inv = lax.rsqrt(jnp.mean(total * total, axis=-1, keepdims=True) + EPSILON)
     o_ref[i] = (total * inv * gain_ref[pl.ds(h, 1), :]).astype(BF)
@@ -203,8 +213,8 @@
     refs = refs[0 if first else 1 :]
     qw_hbm, acc_hbm, p_hbm, gain_ref = refs[:4]
     count = len(order) * PER
-    states = refs[4 : 4 + 2 * count]
-    out_hbm, qw_ref, acc_ref, p_ref, o_ref, sems, out_sems = refs[4 + 2 * count :]
+    states = refs[4 : 4 + 2 * len(order)]
+    out_hbm, qw_ref, acc_ref, p_ref, o_ref, sems, out_sems = refs[4 + 2 * len(order) :]
     loads = []
     for i in range(count):
         h = head_at(pos_ref, order, i)
@@ -252,8 +262,8 @@
 
 def last_kernel(order, pos_ref, prev_hbm, qw_ref, acc_ref, gain_ref, *refs):
     count = len(order) * PER
-    states = refs[: 2 * count]
-    out_hbm, o_ref, out_sems = refs[2 * count :]
+    states = refs[: 2 * len(order)]
+    out_hbm, o_ref, out_sems = refs[2 * len(order) :]
     stores = [
         finish(
             i, head_at(pos_ref, order, i), acc_ref[i], qw_ref.at[i], 0, states, gain_ref, o_ref, out_hbm, out_sems
@@ -295,7 +305,10 @@
     queries, key_vectors, value_vectors = (in_hbm(a) for a in (queries, key_vectors, value_vectors))
     states = call(
         state_kernel, sds((HEADS, DH, DH), BF), [HBM_SPEC] * 2, (2 * tokens * HEADS * DH * DH, 3 << 20),
-        scratch=[pltpu.VMEM(whole, BF), pltpu.VMEM(whole, BF), DMA((2, LOADS))],
+        out_specs=HBM_SPEC,
+        scratch=[
+            pltpu.VMEM(whole, BF), pltpu.VMEM(whole, BF), pltpu.VMEM((HEADS, DH, DH), BF), DMA((2, LOADS)), DMA((LOADS,)),
+        ],
     )(key_vectors, value_vectors)
     gathered = lax.all_to_all(states, "z", split_axis=0, concat_axis=0, tiled=True)
 
@@ -322,26 +335,20 @@
     prefix = lax.all_to_all(prefixes.reshape(HEADS, DH, DH), "z", split_axis=0, concat_axis=0, tiled=True)
     total, sent = call(pair_kernel, (sds(state, F32), sds(state, BF)), [VMEM_SPEC] * 2, (DH * DH, 1 << 18))(mine, other)
     around = to_others(sent, "y")
-    *near, sent = call(
-        near_kernel, (sds((NEAR * DH, DH), BF),) * PER + (sds(state, BF),), [SMEM_SPEC] + [VMEM_SPEC] * 6,
+    near, sent = call(
+        near_kernel, (sds((PER * NEAR * DH, DH), BF), sds(state, BF)), [SMEM_SPEC] + [VMEM_SPEC] * 6,
         (8 * DH * DH, 1 << 18),
     )(pos, mine, other, total, *around)
     around = to_others(sent, "x")
     far = call(
-        far_kernel, (sds((FAR * DH, DH), BF),) * PER, [SMEM_SPEC] + [VMEM_SPEC] * 3, (8 * DH * DH, 1 << 18)
+        far_kernel, sds((PER * FAR * DH, DH), BF), [SMEM_SPEC] + [VMEM_SPEC] * 3, (8 * DH * DH, 1 << 18)
     )(pos, *around)
 
-    near, far = list(near), list(far)
-
-    def paired():
-        return [part[i] for i in range(PER) for part in (near, far)]
-
-    held = [((0,), paired())]
+    held = [((0,), [near, far])]
     for hop in range(1, 5):
-        near = [lax.ppermute(part, ("core", "z"), RING) for part in near]
-        far = [lax.ppermute(part, ("core", "z"), RING) for part in far]
-        arrays = paired()
-        held.append(((hop, -hop), arrays + [swap(a) for a in arrays]) if hop < 4 else ((hop,), arrays))
+        near = lax.ppermute(near, ("core", "z"), RING)
+        far = lax.ppermute(far, ("core", "z"), RING)
+        held.append(((hop, -hop), [near, far, swap(near), swap(far)]) if hop < 4 else ((hop,), [near, far]))
 
     out = None
     for hop in range(2):

time: 101 us -> 87.8 us (0.87)
  starting transfers between devices: 59.6 us -> 45.2 us
  waiting for transfers between devices: 10.7 us -> 12.8 us
    ppermute x16 -> x8, starting transfers between devices: 22.2 us -> 11.5 us  [the longest x4 6.24 us: body(): near = lax.ppermute(near, ('core', 'z'), RING)]
    ppermute x13 -> x7, starting transfers between devices: 14.9 us -> 11.3 us  [swap(): return lax.ppermute(value, 'core', SWAP)]
    ppermute x16 -> x8, waiting for transfers between devices: 0.61 us -> 3.49 us  [the longest x4 2.9 us: body(): far = lax.ppermute(far, ('core', 'z'), RING)]
  transfers between devices with their start and end apart: 37 -> 23, of which waited for: 6 -> 4; matrix products, arithmetic and copies ran while one was open for 0% -> 0% of each run, Pallas kernels for 19% -> 22%
where the time goes in v2:
time: 87.8 us; the launch traced here: 87.5 us
  starting transfers between devices  45.2 us (51%)
  Pallas kernels  24.7 us (28%)
  waiting for transfers between devices  12.8 us (15%)
  local copies, waits for them, and re-layouts  4.21 us (5%)
    ppermute x7, starting transfers between devices, swap(): return lax.ppermute(value, 'core', SWAP)  11.3 us
    all_to_all x1, starting transfers between devices, body(): lax.all_to_all(states, 'z', split_axis=0, concat_axis=0, tiled=True)  9.02 us
    pallas_call x2, Pallas kernels, body(): call(functools.partial(step_kernel, order, out is None), sds(whole, BF),...  6.87 us
    all_to_all x1, waiting for transfers between devices, body(): lax.all_to_all(states, 'z', split_axis=0, concat_axis=0, tiled=True)  6.87 us
    pallas_call x1, Pallas kernels, body(): call(local_kernel, (sds(whole, F32), sds((HEADS, tokens, LEVELS * DH), BF...  6.68 us
    ppermute x4, starting transfers between devices, body(): near = lax.ppermute(near, ('core', 'z'), RING)  6.24 us
    ppermute x4, starting transfers between devices, body(): far = lax.ppermute(far, ('core', 'z'), RING)  5.22 us
    ppermute x2, starting transfers between devices, to_others(): a2 = lax.ppermute(value, axis, shift(4, 2))  5.07 us
  transfers between devices with their start and end apart: 23, of which 4 were waited for; matrix products, arithmetic and copies ran while one was open for 0% of the time, Pallas kernels for 22%

profile of v2, /device:TPU:1, one launch (start us, length us, event | category | flops | bytes accessed | tf_op | source)
XLA Modules:
  0.0 87.5 jit_solution(17376689888412261094)
XLA Ops:
  0.0 2.9 %shard_map.64 = bf16[16,128,128]{2,1,0:T(8,128)(2,1)} custom-call(bf16[256,2048]{1,0:T(8,128)(2,1)} %k_hbm.3, bf16[256,2048]{1,0:T(8,128)(2,1)} %v_hbm.3), custom_call_target="tpu_custom_call" | custom-call | flops 134217728 | bytes 3145728 | tf_op jit(solution)/shard_map/pallas_call | solution.py:306
  3.0 9.0 %all-to-all-start = ((bf16[16,128,128]{2,1,0:T(8,128)(2,1)}), bf16[16,128,128]{2,1,0:T(8,128)(2,1)S(1)}, u32[]{:S(2)}, u32[]{:S(2)}) async-start(bf16[16,128,128]{2,1,0:T(8,128)(2,1)} %shard_map.64), calls=%async_computation | async-start | bytes 1048576 | tf_op jit(solution)/shard_map/all_to_all | solution.py:313
  12.3 6.7 %shard_map.65 = (f32[256,2048]{1,0:T(8,128)S(1)}, bf16[16,256,768]{2,1,0:T(8,128)(2,1)S(1)}) custom-call(bf16[256,2048]{1,0:T(8,128)(2,1)} %q_hbm.1, bf16[256,2048]{1,0:T(8,128)(2,1)} %k_hbm.3, bf16[256,2048]{1,0:T(8,128)(2,1)} %v_hbm.3, s32[6,256]{1,0:T(8,128)S(1)} %dynamic-slice_bitcast_fusion.codes_ref, bf16[128,128]{1,0:T(8,128)(2,1)S(1)} %pad.4.table_ref), custom_call_target="tpu_custom_call" | custom-call | flops 536870912 | bytes 12582912 | tf_op jit(solution)/shard_map/pallas_call | solution.py:318
  19.0 2.6 %copy-done.1 = bf16[16,256,768]{2,1,0:T(8,128)(2,1)} copy-done((bf16[16,256,768]{2,1,0:T(8,128)(2,1)}, bf16[16,256,768]{2,1,0:T(8,128)(2,1)S(1)}, u32[]{:S(2)}) %copy-start.1) | copy-done | bytes 6291480
  21.7 1.4 %copy-done.2 = f32[256,2048]{1,0:T(8,128)} copy-done((f32[256,2048]{1,0:T(8,128)}, f32[256,2048]{1,0:T(8,128)S(1)}, u32[]{:S(2)}) %copy-start.2) | copy-done | bytes 2097176
  23.1 6.9 %all-to-all-done = bf16[16,128,128]{2,1,0:T(8,128)(2,1)S(1)} async-done(((bf16[16,128,128]{2,1,0:T(8,128)(2,1)}), bf16[16,128,128]{2,1,0:T(8,128)(2,1)S(1)}, u32[]{:S(2)}, u32[]{:S(2)}) %all-to-all-start) | async-done | bytes 524320 | tf_op jit(solution)/shard_map/all_to_all | solution.py:313
  30.6 0.9 %shard_map.66 = bf16[8,256,128]{2,1,0:T(8,128)(2,1)} custom-call(bf16[8,256,128]{2,1,0:T(8,128)(2,1)S(1)} %bitcast.9), custom_call_target="tpu_custom_call" | custom-call | flops 262144 | bytes 1048576 | tf_op jit(solution)/shard_map/pallas_call | solution.py:334
  31.5 3.5 %all-to-all-start.1 = ((bf16[16,128,128]{2,1,0:T(8,128)(2,1)}), bf16[16,128,128]{2,1,0:T(8,128)(2,1)S(1)}, u32[]{:S(2)}, u32[]{:S(2)}) async-start(bf16[16,128,128]{2,1,0:T(8,128)(2,1)} %bitcast.6), calls=%async_computation.1 | async-start | bytes 1048576 | tf_op jit(solution)/shard_map/all_to_all | solution.py:335
  35.0 1.4 %collective-permute-start.1 = (bf16[256,128]{1,0:T(8,128)(2,1)S(1)}, bf16[256,128]{1,0:T(8,128)(2,1)S(1)}, u32[]{:S(2)}, u32[]{:S(2)}) collective-permute-start(bf16[256,128]{1,0:T(8,128)(2,1)S(1)} %get-tuple-element.22), channel_id=1, source_target_pairs={{0,16},{16,32},{32,48},{48,0},{1,17},{17,33},{33,49},{49,1},{2,18}... | collective-permute-start | bytes 196616 | tf_op jit(solution)/shard_map/ppermute | solution.py:287
  36.4 2.6 %collective-permute-start.2 = (bf16[256,128]{1,0:T(8,128)(2,1)S(1)}, bf16[256,128]{1,0:T(8,128)(2,1)S(1)}, u32[]{:S(2)}, u32[]{:S(2)}) collective-permute-start(bf16[256,128]{1,0:T(8,128)(2,1)S(1)} %get-tuple-element.22), channel_id=1, source_target_pairs={{0,32},{16,48},{32,0},{48,16},{1,33},{17,49},{33,1},{49,17},{2,34}... | collective-permute-start | bytes 196616 | tf_op jit(solution)/shard_map/ppermute | solution.py:286
  39.0 1.1 %collective-permute-start.3 = (bf16[256,128]{1,0:T(8,128)(2,1)S(1)}, bf16[256,128]{1,0:T(8,128)(2,1)S(1)}, u32[]{:S(2)}, u32[]{:S(2)}) collective-permute-start(bf16[256,128]{1,0:T(8,128)(2,1)S(1)} %get-tuple-element.22), channel_id=1, source_target_pairs={{0,48},{16,0},{32,16},{48,32},{1,49},{17,1},{33,17},{49,33},{2,50}... | collective-permute-start | bytes 196616 | tf_op jit(solution)/shard_map/ppermute | solution.py:288
  40.1 2.4 %collective-permute-done.2.a2_ref = bf16[256,128]{1,0:T(8,128)(2,1)S(1)} collective-permute-done((bf16[256,128]{1,0:T(8,128)(2,1)S(1)}, bf16[256,128]{1,0:T(8,128)(2,1)S(1)}, u32[]{:S(2)}, u32[]{:S(2)}) %collective-permute-start.2) | collective-permute-done | bytes 65568 | tf_op jit(solution)/shard_map/ppermute | solution.py:286
  42.6 0.6 shard_map.69
  43.2 2.5 %collective-permute-start.7 = (bf16[768,128]{1,0:T(8,128)(2,1)S(1)}, bf16[768,128]{1,0:T(8,128)(2,1)S(1)}, u32[]{:S(2)}, u32[]{:S(2)}) collective-permute-start(bf16[768,128]{1,0:T(8,128)(2,1)S(1)} %get-tuple-element.23.refs_4_), channel_id=1, source_target_pairs={{0,1},{1,2},{2,3},{3,4},{4,5},{5,6},{6,7},{7,0},{8,15},{9,8},{10,9... | collective-permute-start | bytes 589832 | tf_op jit(solution)/shard_map/ppermute | solution.py:349
  45.7 1.2 %collective-permute-start.4 = (bf16[256,128]{1,0:T(8,128)(2,1)S(1)}, bf16[256,128]{1,0:T(8,128)(2,1)S(1)}, u32[]{:S(2)}, u32[]{:S(2)}) collective-permute-start(bf16[256,128]{1,0:T(8,128)(2,1)S(1)} %get-tuple-element.24), channel_id=1, source_target_pairs={{0,64},{64,128},{128,192},{192,0},{1,65},{65,129},{129,193},{193,1... | collective-permute-start | bytes 196616 | tf_op jit(solution)/shard_map/ppermute | solution.py:287
  46.9 2.4 %collective-permute-start.5 = (bf16[256,128]{1,0:T(8,128)(2,1)S(1)}, bf16[256,128]{1,0:T(8,128)(2,1)S(1)}, u32[]{:S(2)}, u32[]{:S(2)}) collective-permute-start(bf16[256,128]{1,0:T(8,128)(2,1)S(1)} %get-tuple-element.24), channel_id=1, source_target_pairs={{0,128},{64,192},{128,0},{192,64},{1,129},{65,193},{129,1},{193,65... | collective-permute-start | bytes 196616 | tf_op jit(solution)/shard_map/ppermute | solution.py:286
  49.4 1.2 %collective-permute-start.6 = (bf16[256,128]{1,0:T(8,128)(2,1)S(1)}, bf16[256,128]{1,0:T(8,128)(2,1)S(1)}, u32[]{:S(2)}, u32[]{:S(2)}) collective-permute-start(bf16[256,128]{1,0:T(8,128)(2,1)S(1)} %get-tuple-element.24), channel_id=1, source_target_pairs={{0,192},{64,0},{128,64},{192,128},{1,193},{65,1},{129,65},{193,129... | collective-permute-start | bytes 196616 | tf_op jit(solution)/shard_map/ppermute | solution.py:288
  51.1 2.1 %collective-permute-start.11 = (bf16[768,128]{1,0:T(8,128)(2,1)S(1)}, bf16[768,128]{1,0:T(8,128)(2,1)S(1)}, u32[]{:S(2)}, u32[]{:S(2)}) collective-permute-start(bf16[768,128]{1,0:T(8,128)(2,1)S(1)} %collective-permute-done.7.refs_5_), channel_id=1, source_target_pairs={{0,1},{1,2},{2,3},{3,4},{4,5},{5,6},{6,7},{7,0},{8,15},{9,8},{10,9... | collective-permute-start | bytes 589832 | tf_op jit(solution)/shard_map/ppermute | solution.py:349
  53.2 0.6 shard_map.70.refs_5_
  53.8 1.0 %collective-permute-start.8 = (bf16[512,128]{1,0:T(8,128)(2,1)S(1)}, bf16[512,128]{1,0:T(8,128)(2,1)S(1)}, u32[]{:S(2)}, u32[]{:S(2)}) collective-permute-start(bf16[512,128]{1,0:T(8,128)(2,1)S(1)} %shard_map.70.refs_5_), channel_id=1, source_target_pairs={{0,1},{1,2},{2,3},{3,4},{4,5},{5,6},{6,7},{7,0},{8,15},{9,8},{10,9... | collective-permute-start | bytes 393224 | tf_op jit(solution)/shard_map/ppermute | solution.py:350
  54.8 2.9 %collective-permute-done.8.refs_6_ = bf16[512,128]{1,0:T(8,128)(2,1)S(1)} collective-permute-done((bf16[512,128]{1,0:T(8,128)(2,1)S(1)}, bf16[512,128]{1,0:T(8,128)(2,1)S(1)}, u32[]{:S(2)}, u32[]{:S(2)}) %collective-permute-start.8) | collective-permute-done | bytes 131104 | tf_op jit(solution)/shard_map/ppermute | solution.py:350
  57.7 2.6 %collective-permute-start.12 = (bf16[512,128]{1,0:T(8,128)(2,1)S(1)}, bf16[512,128]{1,0:T(8,128)(2,1)S(1)}, u32[]{:S(2)}, u32[]{:S(2)}) collective-permute-start(bf16[512,128]{1,0:T(8,128)(2,1)S(1)} %collective-permute-done.8.refs_6_), channel_id=1, source_target_pairs={{0,1},{1,2},{2,3},{3,4},{4,5},{5,6},{6,7},{7,0},{8,15},{9,8},{10,9... | collective-permute-start | bytes 393224 | tf_op jit(solution)/shard_map/ppermute | solution.py:350
  60.6 3.2 %collective-permute-start.9 = (bf16[768,128]{1,0:T(8,128)(2,1)S(1)}, bf16[768,128]{1,0:T(8,128)(2,1)S(1)}, u32[]{:S(2)}, u32[]{:S(2)}) collective-permute-start(bf16[768,128]{1,0:T(8,128)(2,1)S(1)} %collective-permute-done.7.refs_5_), channel_id=1, source_target_pairs={{0,8},{8,0},{1,9},{9,1},{2,10},{10,2},{3,11},{11,3},{4,12},{12,4},... | collective-permute-start | bytes 589832 | tf_op jit(solution)/shard_map/ppermute | solution.py:293
  63.8 1.6 %collective-permute-start.16 = (bf16[512,128]{1,0:T(8,128)(2,1)S(1)}, bf16[512,128]{1,0:T(8,128)(2,1)S(1)}, u32[]{:S(2)}, u32[]{:S(2)}) collective-permute-start(bf16[512,128]{1,0:T(8,128)(2,1)S(1)} %collective-permute-done.12.refs_1_), channel_id=1, source_target_pairs={{0,1},{1,2},{2,3},{3,4},{4,5},{5,6},{6,7},{7,0},{8,15},{9,8},{10,9... | collective-permute-start | bytes 393224 | tf_op jit(solution)/shard_map/ppermute | solution.py:350
  65.4 2.8 %collective-permute-start.14 = (bf16[512,128]{1,0:T(8,128)(2,1)S(1)}, bf16[512,128]{1,0:T(8,128)(2,1)S(1)}, u32[]{:S(2)}, u32[]{:S(2)}) collective-permute-start(bf16[512,128]{1,0:T(8,128)(2,1)S(1)} %collective-permute-done.12.refs_1_), channel_id=1, source_target_pairs={{0,8},{8,0},{1,9},{9,1},{2,10},{10,2},{3,11},{11,3},{4,12},{12,4},... | collective-permute-start | bytes 393224 | tf_op jit(solution)/shard_map/ppermute | solution.py:293
  68.3 2.0 %collective-permute-start.17 = (bf16[768,128]{1,0:T(8,128)(2,1)S(1)}, bf16[768,128]{1,0:T(8,128)(2,1)S(1)}, u32[]{:S(2)}, u32[]{:S(2)}) collective-permute-start(bf16[768,128]{1,0:T(8,128)(2,1)S(1)} %collective-permute-done.15.refs_4_), channel_id=1, source_target_pairs={{0,8},{8,0},{1,9},{9,1},{2,10},{10,2},{3,11},{11,3},{4,12},{12,4},... | collective-permute-start | bytes 589832 | tf_op jit(solution)/shard_map/ppermute | solution.py:293
  70.3 1.4 %collective-permute-start.19 = (bf16[768,128]{1,0:T(8,128)(2,1)S(1)}, bf16[768,128]{1,0:T(8,128)(2,1)S(1)}, u32[]{:S(2)}, u32[]{:S(2)}) collective-permute-start(bf16[768,128]{1,0:T(8,128)(2,1)S(1)} %collective-permute-done.15.refs_4_), channel_id=1, source_target_pairs={{0,1},{1,2},{2,3},{3,4},{4,5},{5,6},{6,7},{7,0},{8,15},{9,8},{10,9... | collective-permute-start | bytes 589832 | tf_op jit(solution)/shard_map/ppermute | solution.py:349
  71.6 2.7 %collective-permute-start.18 = (bf16[512,128]{1,0:T(8,128)(2,1)S(1)}, bf16[512,128]{1,0:T(8,128)(2,1)S(1)}, u32[]{:S(2)}, u32[]{:S(2)}) collective-permute-start(bf16[512,128]{1,0:T(8,128)(2,1)S(1)} %collective-permute-done.16.refs_5_), channel_id=1, source_target_pairs={{0,8},{8,0},{1,9},{9,1},{2,10},{10,2},{3,11},{11,3},{4,12},{12,4},... | collective-permute-start | bytes 393224 | tf_op jit(solution)/shard_map/ppermute | solution.py:293
  74.4 3.6 %shard_map.73 = (bf16[10,256,640]{2,1,0:T(8,128)(2,1)S(1)}, f32[10,256,128]{2,1,0:T(8,128)S(1)}) custom-call(s32[4]{0:T(128)S(1)} %pad_add_fusion.pos_ref, bf16[16,256,768]{2,1,0:T(8,128)(2,1)} %copy-done.1, f32[256,2048]{1,0:T(8,128)} %copy-done.2, bf16[16,128,128]{2,1,0:T(8,128)(2,1)S(1)} %all-to-all-done.1.refs_2_.refs_3_.p_hbm), custom_call_target="tpu_custom_call" | custom-call | flops 83886080 | bytes 5242880 | tf_op jit(solution)/shard_map/pallas_call | solution.py:371
  78.0 3.0 %shard_map.71.refs_0_ = bf16[256,2048]{1,0:T(8,128)(2,1)} custom-call(s32[4]{0:T(128)S(1)} %pad_add_fusion.pos_ref, bf16[16,256,768]{2,1,0:T(8,128)(2,1)} %copy-done.1, f32[256,2048]{1,0:T(8,128)} %copy-done.2, bf16[16,128,128]{2,1,0:T(8,128)(2,1)S(1)} %all-to-all-done.1.refs_2_.refs_3_.p_hbm, f32[16,128]{1,0:T(8,128)S(1)} %copy-done.3, ...), custom_call_target="tpu_custom_call" | custom-call | flops 100663296 | bytes 1048576 | tf_op jit(solution)/shard_map/pallas_call | solution.py:357
  81.0 3.9 %shard_map.72.prev_hbm = bf16[256,2048]{1,0:T(8,128)(2,1)} custom-call(s32[4]{0:T(128)S(1)} %pad_add_fusion.pos_ref, bf16[256,2048]{1,0:T(8,128)(2,1)} %shard_map.71.refs_0_, bf16[16,256,768]{2,1,0:T(8,128)(2,1)} %copy-done.1, f32[256,2048]{1,0:T(8,128)} %copy-done.2, ...), custom_call_target="tpu_custom_call", output_to_operand_aliasing={{}: (1, {})} | custom-call | flops 201326592 | bytes 2097152 | tf_op jit(solution)/shard_map/pallas_call | solution.py:357
  84.9 2.4 %shard_map.74 = bf16[256,2048]{1,0:T(8,128)(2,1)} custom-call(s32[4]{0:T(128)S(1)} %pad_add_fusion.pos_ref, bf16[256,2048]{1,0:T(8,128)(2,1)} %shard_map.72.prev_hbm, bf16[10,256,640]{2,1,0:T(8,128)(2,1)S(1)} %get-tuple-element.25.qw_ref, f32[10,256,128]{2,1,0:T(8,128)S(1)} %get-tuple-element.26.acc_ref, ...), custom_call_target="tpu_custom_call", output_to_operand_aliasing={{}: (1, {})} | custom-call | flops 419430400 | bytes 5242880 | tf_op jit(solution)/shard_map/pallas_call | solution.py:377
  (42 shorter events, 2.1 us)
Async XLA Ops:
  0.0 12.3 %copy-start = (s32[2048,6]{0,1:T(8,128)S(1)}, s32[2048,6]{0,1:T(8,128)}, u32[]{:S(2)}) copy-start(s32[2048,6]{0,1:T(8,128)} %param.9) | copy-start | bytes 147460
  0.0 12.1 %copy-start.4 = (bf16[16,16]{1,0:T(8,128)(2,1)S(1)}, bf16[16,16]{1,0:T(8,128)(2,1)}, u32[]{:S(2)}) copy-start(bf16[16,16]{1,0:T(8,128)(2,1)} %param.10) | copy-start | bytes 1540
  3.0 27.0 %all-to-all-start = ((bf16[16,128,128]{2,1,0:T(8,128)(2,1)}), bf16[16,128,128]{2,1,0:T(8,128)(2,1)S(1)}, u32[]{:S(2)}, u32[]{:S(2)}) async-start(bf16[16,128,128]{2,1,0:T(8,128)(2,1)} %shard_map.64), calls=%async_computation | async-start | bytes 1048576 | tf_op jit(solution)/shard_map/all_to_all | solution.py:313
  19.0 2.6 %copy-start.1 = (bf16[16,256,768]{2,1,0:T(8,128)(2,1)}, bf16[16,256,768]{2,1,0:T(8,128)(2,1)S(1)}, u32[]{:S(2)}) copy-start(bf16[16,256,768]{2,1,0:T(8,128)(2,1)S(1)} %get-tuple-element.18.refs_0_.refs_1_.qw_hbm) | copy-start | bytes 18874372
  21.7 1.4 %copy-start.2 = (f32[256,2048]{1,0:T(8,128)}, f32[256,2048]{1,0:T(8,128)S(1)}, u32[]{:S(2)}) copy-start(f32[256,2048]{1,0:T(8,128)S(1)} %get-tuple-element.19.refs_1_.refs_2_.acc_hbm) | copy-start | bytes 6291460
  30.0 5.0 %collective-permute-start = (f32[256,128]{1,0:T(8,128)S(1)}, f32[256,128]{1,0:T(8,128)S(1)}, u32[]{:S(2)}, u32[]{:S(2)}) collective-permute-start(f32[256,128]{1,0:T(8,128)S(1)} %shard_map.67.mine_ref), channel_id=1, source_target_pairs={{0,8},{8,0},{1,9},{9,1},{2,10},{10,2},{3,11},{11,3},{4,12},{12,4},... | collective-permute-start | bytes 393224 | tf_op jit(solution)/shard_map/ppermute | solution.py:293
  31.5 42.9 %all-to-all-start.1 = ((bf16[16,128,128]{2,1,0:T(8,128)(2,1)}), bf16[16,128,128]{2,1,0:T(8,128)(2,1)S(1)}, u32[]{:S(2)}, u32[]{:S(2)}) async-start(bf16[16,128,128]{2,1,0:T(8,128)(2,1)} %bitcast.6), calls=%async_computation.1 | async-start | bytes 1048576 | tf_op jit(solution)/shard_map/all_to_all | solution.py:335
  35.0 5.1 %collective-permute-start.1 = (bf16[256,128]{1,0:T(8,128)(2,1)S(1)}, bf16[256,128]{1,0:T(8,128)(2,1)S(1)}, u32[]{:S(2)}, u32[]{:S(2)}) collective-permute-start(bf16[256,128]{1,0:T(8,128)(2,1)S(1)} %get-tuple-element.22), channel_id=1, source_target_pairs={{0,16},{16,32},{32,48},{48,0},{1,17},{17,33},{33,49},{49,1},{2,18}... | collective-permute-start | bytes 196616 | tf_op jit(solution)/shard_map/ppermute | solution.py:287
  36.4 6.2 %collective-permute-start.2 = (bf16[256,128]{1,0:T(8,128)(2,1)S(1)}, bf16[256,128]{1,0:T(8,128)(2,1)S(1)}, u32[]{:S(2)}, u32[]{:S(2)}) collective-permute-start(bf16[256,128]{1,0:T(8,128)(2,1)S(1)} %get-tuple-element.22), channel_id=1, source_target_pairs={{0,32},{16,48},{32,0},{48,16},{1,33},{17,49},{33,1},{49,17},{2,34}... | collective-permute-start | bytes 196616 | tf_op jit(solution)/shard_map/ppermute | solution.py:286
  39.0 3.6 %collective-permute-start.3 = (bf16[256,128]{1,0:T(8,128)(2,1)S(1)}, bf16[256,128]{1,0:T(8,128)(2,1)S(1)}, u32[]{:S(2)}, u32[]{:S(2)}) collective-permute-start(bf16[256,128]{1,0:T(8,128)(2,1)S(1)} %get-tuple-element.22), channel_id=1, source_target_pairs={{0,48},{16,0},{32,16},{48,32},{1,49},{17,1},{33,17},{49,33},{2,50}... | collective-permute-start | bytes 196616 | tf_op jit(solution)/shard_map/ppermute | solution.py:288
  43.2 7.9 %collective-permute-start.7 = (bf16[768,128]{1,0:T(8,128)(2,1)S(1)}, bf16[768,128]{1,0:T(8,128)(2,1)S(1)}, u32[]{:S(2)}, u32[]{:S(2)}) collective-permute-start(bf16[768,128]{1,0:T(8,128)(2,1)S(1)} %get-tuple-element.23.refs_4_), channel_id=1, source_target_pairs={{0,1},{1,2},{2,3},{3,4},{4,5},{5,6},{6,7},{7,0},{8,15},{9,8},{10,9... | collective-permute-start | bytes 589832 | tf_op jit(solution)/shard_map/ppermute | solution.py:349
  45.7 7.5 %collective-permute-start.4 = (bf16[256,128]{1,0:T(8,128)(2,1)S(1)}, bf16[256,128]{1,0:T(8,128)(2,1)S(1)}, u32[]{:S(2)}, u32[]{:S(2)}) collective-permute-start(bf16[256,128]{1,0:T(8,128)(2,1)S(1)} %get-tuple-element.24), channel_id=1, source_target_pairs={{0,64},{64,128},{128,192},{192,0},{1,65},{65,129},{129,193},{193,1... | collective-permute-start | bytes 196616 | tf_op jit(solution)/shard_map/ppermute | solution.py:287
  46.9 6.3 %collective-permute-start.5 = (bf16[256,128]{1,0:T(8,128)(2,1)S(1)}, bf16[256,128]{1,0:T(8,128)(2,1)S(1)}, u32[]{:S(2)}, u32[]{:S(2)}) collective-permute-start(bf16[256,128]{1,0:T(8,128)(2,1)S(1)} %get-tuple-element.24), channel_id=1, source_target_pairs={{0,128},{64,192},{128,0},{192,64},{1,129},{65,193},{129,1},{193,65... | collective-permute-start | bytes 196616 | tf_op jit(solution)/shard_map/ppermute | solution.py:286
  49.4 3.8 %collective-permute-start.6 = (bf16[256,128]{1,0:T(8,128)(2,1)S(1)}, bf16[256,128]{1,0:T(8,128)(2,1)S(1)}, u32[]{:S(2)}, u32[]{:S(2)}) collective-permute-start(bf16[256,128]{1,0:T(8,128)(2,1)S(1)} %get-tuple-element.24), channel_id=1, source_target_pairs={{0,192},{64,0},{128,64},{192,128},{1,193},{65,1},{129,65},{193,129... | collective-permute-start | bytes 196616 | tf_op jit(solution)/shard_map/ppermute | solution.py:288
  51.1 9.2 %collective-permute-start.11 = (bf16[768,128]{1,0:T(8,128)(2,1)S(1)}, bf16[768,128]{1,0:T(8,128)(2,1)S(1)}, u32[]{:S(2)}, u32[]{:S(2)}) collective-permute-start(bf16[768,128]{1,0:T(8,128)(2,1)S(1)} %collective-permute-done.7.refs_5_), channel_id=1, source_target_pairs={{0,1},{1,2},{2,3},{3,4},{4,5},{5,6},{6,7},{7,0},{8,15},{9,8},{10,9... | collective-permute-start | bytes 589832 | tf_op jit(solution)/shard_map/ppermute | solution.py:349
  53.8 24.2 %copy-start.3 = (f32[16,128]{1,0:T(8,128)S(1)}, f32[16,128]{1,0:T(8,128)}, u32[]{:S(2)}) copy-start(f32[16,128]{1,0:T(8,128)} %gain_ref.1) | copy-start | bytes 24580
  53.8 3.9 %collective-permute-start.8 = (bf16[512,128]{1,0:T(8,128)(2,1)S(1)}, bf16[512,128]{1,0:T(8,128)(2,1)S(1)}, u32[]{:S(2)}, u32[]{:S(2)}) collective-permute-start(bf16[512,128]{1,0:T(8,128)(2,1)S(1)} %shard_map.70.refs_5_), channel_id=1, source_target_pairs={{0,1},{1,2},{2,3},{3,4},{4,5},{5,6},{6,7},{7,0},{8,15},{9,8},{10,9... | collective-permute-start | bytes 393224 | tf_op jit(solution)/shard_map/ppermute | solution.py:350
  57.7 6.0 %collective-permute-start.12 = (bf16[512,128]{1,0:T(8,128)(2,1)S(1)}, bf16[512,128]{1,0:T(8,128)(2,1)S(1)}, u32[]{:S(2)}, u32[]{:S(2)}) collective-permute-start(bf16[512,128]{1,0:T(8,128)(2,1)S(1)} %collective-permute-done.8.refs_6_), channel_id=1, source_target_pairs={{0,1},{1,2},{2,3},{3,4},{4,5},{5,6},{6,7},{7,0},{8,15},{9,8},{10,9... | collective-permute-start | bytes 393224 | tf_op jit(solution)/shard_map/ppermute | solution.py:350
  60.4 7.9 %collective-permute-start.15 = (bf16[768,128]{1,0:T(8,128)(2,1)S(1)}, bf16[768,128]{1,0:T(8,128)(2,1)S(1)}, u32[]{:S(2)}, u32[]{:S(2)}) collective-permute-start(bf16[768,128]{1,0:T(8,128)(2,1)S(1)} %collective-permute-done.11.refs_0_), channel_id=1, source_target_pairs={{0,1},{1,2},{2,3},{3,4},{4,5},{5,6},{6,7},{7,0},{8,15},{9,8},{10,9... | collective-permute-start | bytes 589832 | tf_op jit(solution)/shard_map/ppermute | solution.py:349
  60.6 9.7 %collective-permute-start.9 = (bf16[768,128]{1,0:T(8,128)(2,1)S(1)}, bf16[768,128]{1,0:T(8,128)(2,1)S(1)}, u32[]{:S(2)}, u32[]{:S(2)}) collective-permute-start(bf16[768,128]{1,0:T(8,128)(2,1)S(1)} %collective-permute-done.7.refs_5_), channel_id=1, source_target_pairs={{0,8},{8,0},{1,9},{9,1},{2,10},{10,2},{3,11},{11,3},{4,12},{12,4},... | collective-permute-start | bytes 589832 | tf_op jit(solution)/shard_map/ppermute | solution.py:293
  63.8 4.4 %collective-permute-start.10 = (bf16[512,128]{1,0:T(8,128)(2,1)S(1)}, bf16[512,128]{1,0:T(8,128)(2,1)S(1)}, u32[]{:S(2)}, u32[]{:S(2)}) collective-permute-start(bf16[512,128]{1,0:T(8,128)(2,1)S(1)} %collective-permute-done.8.refs_6_), channel_id=1, source_target_pairs={{0,8},{8,0},{1,9},{9,1},{2,10},{10,2},{3,11},{11,3},{4,12},{12,4},... | collective-permute-start | bytes 393224 | tf_op jit(solution)/shard_map/ppermute | solution.py:293
  63.8 7.9 %collective-permute-start.16 = (bf16[512,128]{1,0:T(8,128)(2,1)S(1)}, bf16[512,128]{1,0:T(8,128)(2,1)S(1)}, u32[]{:S(2)}, u32[]{:S(2)}) collective-permute-start(bf16[512,128]{1,0:T(8,128)(2,1)S(1)} %collective-permute-done.12.refs_1_), channel_id=1, source_target_pairs={{0,1},{1,2},{2,3},{3,4},{4,5},{5,6},{6,7},{7,0},{8,15},{9,8},{10,9... | collective-permute-start | bytes 393224 | tf_op jit(solution)/shard_map/ppermute | solution.py:350
  65.4 9.0 %collective-permute-start.14 = (bf16[512,128]{1,0:T(8,128)(2,1)S(1)}, bf16[512,128]{1,0:T(8,128)(2,1)S(1)}, u32[]{:S(2)}, u32[]{:S(2)}) collective-permute-start(bf16[512,128]{1,0:T(8,128)(2,1)S(1)} %collective-permute-done.12.refs_1_), channel_id=1, source_target_pairs={{0,8},{8,0},{1,9},{9,1},{2,10},{10,2},{3,11},{11,3},{4,12},{12,4},... | collective-permute-start | bytes 393224 | tf_op jit(solution)/shard_map/ppermute | solution.py:293
  68.2 16.7 %collective-permute-start.13 = (bf16[768,128]{1,0:T(8,128)(2,1)S(1)}, bf16[768,128]{1,0:T(8,128)(2,1)S(1)}, u32[]{:S(2)}, u32[]{:S(2)}) collective-permute-start(bf16[768,128]{1,0:T(8,128)(2,1)S(1)} %collective-permute-done.11.refs_0_), channel_id=1, source_target_pairs={{0,8},{8,0},{1,9},{9,1},{2,10},{10,2},{3,11},{11,3},{4,12},{12,4},... | collective-permute-start | bytes 589832 | tf_op jit(solution)/shard_map/ppermute | solution.py:293
  68.3 16.7 %collective-permute-start.17 = (bf16[768,128]{1,0:T(8,128)(2,1)S(1)}, bf16[768,128]{1,0:T(8,128)(2,1)S(1)}, u32[]{:S(2)}, u32[]{:S(2)}) collective-permute-start(bf16[768,128]{1,0:T(8,128)(2,1)S(1)} %collective-permute-done.15.refs_4_), channel_id=1, source_target_pairs={{0,8},{8,0},{1,9},{9,1},{2,10},{10,2},{3,11},{11,3},{4,12},{12,4},... | collective-permute-start | bytes 589832 | tf_op jit(solution)/shard_map/ppermute | solution.py:293
  70.3 14.7 %collective-permute-start.19 = (bf16[768,128]{1,0:T(8,128)(2,1)S(1)}, bf16[768,128]{1,0:T(8,128)(2,1)S(1)}, u32[]{:S(2)}, u32[]{:S(2)}) collective-permute-start(bf16[768,128]{1,0:T(8,128)(2,1)S(1)} %collective-permute-done.15.refs_4_), channel_id=1, source_target_pairs={{0,1},{1,2},{2,3},{3,4},{4,5},{5,6},{6,7},{7,0},{8,15},{9,8},{10,9... | collective-permute-start | bytes 589832 | tf_op jit(solution)/shard_map/ppermute | solution.py:349
  71.6 13.3 %collective-permute-start.18 = (bf16[512,128]{1,0:T(8,128)(2,1)S(1)}, bf16[512,128]{1,0:T(8,128)(2,1)S(1)}, u32[]{:S(2)}, u32[]{:S(2)}) collective-permute-start(bf16[512,128]{1,0:T(8,128)(2,1)S(1)} %collective-permute-done.16.refs_5_), channel_id=1, source_target_pairs={{0,8},{8,0},{1,9},{9,1},{2,10},{10,2},{3,11},{11,3},{4,12},{12,4},... | collective-permute-start | bytes 393224 | tf_op jit(solution)/shard_map/ppermute | solution.py:293
  74.3 10.6 %collective-permute-start.20 = (bf16[512,128]{1,0:T(8,128)(2,1)S(1)}, bf16[512,128]{1,0:T(8,128)(2,1)S(1)}, u32[]{:S(2)}, u32[]{:S(2)}) collective-permute-start(bf16[512,128]{1,0:T(8,128)(2,1)S(1)} %collective-permute-done.16.refs_5_), channel_id=1, source_target_pairs={{0,1},{1,2},{2,3},{3,4},{4,5},{5,6},{6,7},{7,0},{8,15},{9,8},{10,9... | collective-permute-start | bytes 393224 | tf_op jit(solution)/shard_map/ppermute | solution.py:350
